TPU v7x, 256 devices: a whole 4x4x8 slice. The times are simulated.
256 devices in a mesh: dp: 32 (over x, y, core), mp: 8 (over z).
Axes of the slice: x: 4, y: 4, z: 8, core: 2. Of those that a mesh axis runs over, the one named last changes fastest.
Arguments:
- features: bfloat16 [65536, 2, 512], P('dp'), may hold values from -27 to 27
- projection: bfloat16 [512, 256], replicated, may hold values from -1 to 1
- prototypes: float32 [3000, 256], P('mp'), may hold values from -7 to 7
Outputs:
- grad_prototypes: float32 [3000, 256], P('mp')
- grad_projection: float32 [512, 256], replicated
- loss: float32 [], replicated
All inputs are finite; a program needn't handle non-finite values.
Results may differ from a plain program's by a relative error of at most 0.0019.
The roundings to bfloat16 on the way count: a program that leaves them out, or rounds other values in their place, can miss the bound.
Values may be sent and summed in bfloat16 or wider, within the bound.
A program may use at most 128 MiB of HBM per device.

v0:
```python
import jax
import jax.numpy as jnp
from jax import lax
from jax.sharding import PartitionSpec as P

ITERS = 3


EPSILON_CODES = 0.05
SOFTMAX_TEMPER = 0.1
LOSS_FACTOR = 4096.0
TINY = 1e-06


def unit_rows(values):
    inverse = lax.rsqrt(jnp.sum(values * values, axis=-1, keepdims=True) + TINY)
    return (values * inverse, inverse)


def prototype_totals(values):
    return lax.psum(jnp.sum(values, axis=0), "dp")


def code_totals(values):
    return lax.psum(jnp.sum(values, axis=-1), "mp")


def loss_pieces(
    prototype_logits, softmax_exponent, softmax_denominator, assignments, gradient_factor
):
    swapped_targets = assignments[:, ::-1]
    grad_half = (
        (softmax_exponent / softmax_denominator[..., None] - swapped_targets) * gradient_factor
    ).astype(jnp.bfloat16)
    loss_portion = jnp.sum(
        swapped_targets
        * (prototype_logits * (1.0 / SOFTMAX_TEMPER) - jnp.log(softmax_denominator)[..., None])
    )
    return (grad_half, loss_portion)


def embed_backward(grad_unit, embed_unit, embed_inverse, own_feats):
    along_unit = jnp.sum(embed_unit * grad_unit, axis=-1, keepdims=True)
    grad_raw = ((grad_unit - embed_unit * along_unit) * embed_inverse).astype(jnp.bfloat16)
    return jnp.einsum("bve,bvp->ep", own_feats, grad_raw, preferred_element_type=jnp.float32)


def body(features, projection, prototypes):
    local_rows = features.shape[0]
    own_count = local_rows // lax.axis_size("mp")
    batch_row_count = local_rows * lax.axis_size("dp")
    gradient_factor = LOSS_FACTOR / (2.0 * batch_row_count * SOFTMAX_TEMPER)
    proto_unit, proto_inverse = unit_rows(prototypes)
    proto_half = proto_unit.astype(jnp.bfloat16)
    first_row = lax.axis_index("mp") * own_count
    own_feats = lax.dynamic_slice_in_dim(features, first_row, own_count, 0)
    raw_embed = jnp.einsum("bve,ep->bvp", own_feats, projection, preferred_element_type=jnp.float32)
    embed_unit, embed_inverse = unit_rows(raw_embed)
    embed_half = embed_unit.astype(jnp.bfloat16)
    all_embed = lax.all_gather(embed_half, "mp", axis=0, tiled=True)
    prototype_logits = jnp.einsum(
        "bvp,kp->bvk", all_embed, proto_half, preferred_element_type=jnp.float32
    )
    transport = jnp.exp(prototype_logits * (1.0 / EPSILON_CODES))
    softmax_exponent = jnp.exp(prototype_logits * (1.0 / SOFTMAX_TEMPER))
    soft_part = jnp.sum(softmax_exponent, axis=-1)
    for iteration in range(ITERS - 1):
        transport = transport / prototype_totals(transport)[None]
        transport = transport / code_totals(transport)[..., None]
    transport = transport / prototype_totals(transport)[None]
    softmax_denominator = lax.psum(soft_part, "mp")
    row_sums = code_totals(transport)
    assignments = transport / row_sums[..., None]
    grad_half, loss_portion = loss_pieces(
        prototype_logits, softmax_exponent, softmax_denominator, assignments, gradient_factor
    )
    proto_grad = jnp.einsum("bvk,bvp->kp", grad_half, all_embed, preferred_element_type=jnp.float32)
    proto_grad = lax.psum(proto_grad, "dp")
    grad_unit = lax.psum_scatter(
        jnp.einsum("bvk,kp->bvp", grad_half, proto_half, preferred_element_type=jnp.float32),
        "mp",
        scatter_dimension=0,
        tiled=True,
    )
    weight_part = embed_backward(grad_unit, embed_unit, embed_inverse, own_feats)
    weight_grad, loss_total = lax.psum((weight_part, loss_portion), ("dp", "mp"))
    along_proto = jnp.sum(proto_unit * proto_grad, axis=-1, keepdims=True)
    grad_protos = (proto_grad - proto_unit * along_proto) * proto_inverse
    loss_value = -loss_total / (2.0 * batch_row_count)
    return (grad_protos, weight_grad, loss_value)


def solution(mesh):
    return jax.shard_map(
        body,
        mesh=mesh,
        in_specs=(P("dp", None, None), P(), P("mp", None)),
        out_specs=(P("mp", None), P(), P()),
        check_vma=False,
    )
```

profile of v0, /device:TPU:1, one launch (start us, length us, event | category | flops | bytes accessed | tf_op | source)
XLA Modules:
  0.0 803.0 jit_solution(7048572155357733132)
XLA Ops:
  7.2 1.4 constant_dynamic-slice_fusion
  8.7 0.8 copy-done.3
  9.5 0.4 multiply_reduce_fusion.1
  9.9 0.7 multiply_convert_fusion.1
  10.7 1.1 multiply_reduce_fusion.4
  11.8 46.3 %all-gather.2.cloned.1.call-done = bf16[2048,2,256]{0,2,1:T(8,128)(2,1)} async-done(((bf16[256,2,256]{0,2,1:T(8,128)(2,1)}), bf16[2048,2,256]{0,2,1:T(8,128)(2,1)}) %all-gather.2.cloned.1.call-update) | async-done | bytes 2097168 | tf_op jit(solution)/shard_map/all_gather | solution.py:60
  58.1 5.4 fusion.12
  63.6 67.0 %psum.71 = f32[2,375]{1,0:T(2,128)S(1)} all-reduce(f32[2,375]{1,0:T(2,128)S(1)} %get-tuple-element.11), channel_id=1, replica_groups=mesh['dp'=32,'mp'=8] {'dp'}, use_global_device_ids=true, to_apply=%region_5.0 | all-reduce | flops 750 | bytes 6000 | tf_op jit(solution)/shard_map/psum | solution.py:21
  130.5 3.8 exponential_reduce_fusion
  134.4 22.2 %psum.72 = f32[2048,2]{0,1:T(2,128)S(1)} all-reduce(f32[2048,2]{0,1:T(2,128)S(1)} %get-tuple-element.4), channel_id=1, replica_groups=mesh['dp'=32,'mp'=8] {'mp'}, use_global_device_ids=true, to_apply=%region_7.0 | all-reduce | flops 4096 | bytes 32768 | tf_op jit(solution)/shard_map/psum | solution.py:25
  156.6 4.4 fusion.8
  161.0 69.7 %psum.73 = f32[2,375]{1,0:T(2,128)S(1)} all-reduce(f32[2,375]{1,0:T(2,128)S(1)} %fusion.8), channel_id=1, replica_groups=mesh['dp'=32,'mp'=8] {'dp'}, use_global_device_ids=true, to_apply=%region_9.0 | all-reduce | flops 750 | bytes 6000 | tf_op jit(solution)/shard_map/psum | solution.py:21
  230.7 3.7 fusion.9
  234.4 20.4 %psum.74 = f32[2048,2]{0,1:T(2,128)S(1)} all-reduce(f32[2048,2]{0,1:T(2,128)S(1)} %fusion.9), channel_id=1, replica_groups=mesh['dp'=32,'mp'=8] {'mp'}, use_global_device_ids=true, to_apply=%region_11.0 | all-reduce | flops 4096 | bytes 32768 | tf_op jit(solution)/shard_map/psum | solution.py:25
  254.8 3.9 fusion.10
  258.7 69.3 %psum.75 = f32[2,375]{1,0:T(2,128)S(1)} all-reduce(f32[2,375]{1,0:T(2,128)S(1)} %fusion.10), channel_id=1, replica_groups=mesh['dp'=32,'mp'=8] {'dp'}, use_global_device_ids=true, to_apply=%region_13.0 | all-reduce | flops 750 | bytes 6000 | tf_op jit(solution)/shard_map/psum | solution.py:21
  328.1 4.3 fusion.11
  332.4 20.7 %all-reduce = (f32[2048,2]{0,1:T(2,128)S(1)}, f32[2048,2]{0,1:T(2,128)S(1)}) all-reduce(f32[2048,2]{0,1:T(2,128)S(1)} %fusion.11, f32[2048,2]{0,1:T(2,128)S(1)} %get-tuple-element.3), channel_id=1, replica_groups=mesh['dp'=32,'mp'=8] {'mp'}, use_global_device_ids=true, to_apply=%region_15.0 | all-reduce | flops 8192 | bytes 65536 | tf_op jit(solution)/shard_map/psum | solution.py:25
  353.1 5.1 fusion.7
  358.2 2.6 multiply_reduce_fusion
  360.8 1.6 copy-done.1
  362.4 3.3 fusion.28
  365.8 0.0 all-reduce.4.cloned.1.call-start
  365.8 4.3 convolution_bitcast_fusion.1
  370.2 0.0 all-reduce.6.cloned.1.call-start
  370.3 80.0 %psum.79 = f32[]{:T(128)} all-reduce(f32[]{:T(128)} %get-tuple-element.7), channel_id=1, replica_groups=mesh['dp'=32,'mp'=8] {'dp','mp'}, use_global_device_ids=true, to_apply=%region_22.0 | all-reduce | flops 1 | bytes 8 | tf_op jit(solution)/shard_map/psum | solution.py:86
  450.9 2.5 convolution_bitcast_fusion
  453.4 84.0 %all-reduce.4.cloned.1.call-done = f32[375,256]{1,0:T(8,128)} async-done(((f32[375,256]{1,0:T(8,128)}), f32[375,256]{1,0:T(8,128)}) %all-reduce.4.cloned.1.call-update) | async-done | bytes 384016 | tf_op jit(solution)/shard_map/psum | solution.py:78
  537.5 1.2 multiply_reduce_fusion.3
  538.7 1.9 subtract_multiply_fusion
  540.6 252.9 %all-reduce.6.cloned.1.call-done = f32[512,256]{1,0:T(8,128)} async-done(((f32[512,256]{1,0:T(8,128)}), f32[512,256]{1,0:T(8,128)}) %all-reduce.6.cloned.1.call-update) | async-done | bytes 524304 | tf_op jit(solution)/shard_map/psum | solution.py:86
  793.5 1.9 copy.29
  (23 shorter events, 0.2 us)
Async XLA Ops:
  7.2 2.3 copy-start
  7.2 50.9 %all-gather.2.cloned.1.call-start = ((), (), s32[]{:S(2)}) async-start(), calls=%async_computation.1 | async-start | bytes 2359296 | tf_op jit(solution)/shard_map/all_gather | solution.py:60
  8.7 0.8 copy-start.3
  10.6 440.3 %reduce-scatter.2.cloned.1.call-start = ((), (), s32[]{:S(2)}) async-start(), calls=%async_computation.3 | async-start | bytes 4718592 | tf_op jit(solution)/shard_map/reduce_scatter | solution.py:79
  328.1 30.1 %slice-start = ((s8[6160384]{0:T(1024)(128)(4,1)}), s8[1966080]{0:T(1024)(128)(4,1)S(1)}, s32[]{:S(2)}) async-start(s8[6160384]{0:T(1024)(128)(4,1)} %bitcast.19), calls=%async_computation.5 | async-start | bytes 3932160
  353.1 5.1 slice-start.1
  358.2 4.2 copy-start.2
  360.8 1.6 copy-start.1
  365.8 85.1 %copy-start.4 = (bf16[256,2,512]{2,1,0:T(2,128)(2,1)S(1)}, bf16[256,2,512]{2,1,0:T(2,128)(2,1)}, u32[]{:S(2)}) copy-start(bf16[256,2,512]{2,1,0:T(2,128)(2,1)} %copy-done.3) | copy-start | bytes 1572868
  365.8 171.7 %all-reduce.4.cloned.1.call-start = ((), (), s32[]{:S(2)}) async-start(), calls=%async_computation.2 | async-start | bytes 770048 | tf_op jit(solution)/shard_map/psum | solution.py:78
  370.2 423.3 %all-reduce.6.cloned.1.call-start = ((), (), s32[]{:S(2)}) async-start(), calls=%async_computation.4 | async-start | bytes 1048576 | tf_op jit(solution)/shard_map/psum | solution.py:86
Sparse Core Ops, SparseCore 0:
  10.7 47.3 all-gather.1
  365.9 56.2 reduce-scatter.1
  426.1 111.3 all-reduce.3
  543.4 250.0 all-reduce.5
where the time goes:
time: 804 us; the launch traced here: 803 us
  waiting for transfers between devices  383 us (48%)
  blocking collectives  349 us (43%)
  other arithmetic  32.9 us (4%)
  matrix products  16 us (2%)
  between operations  15.7 us (2%)
    psum x1, waiting for transfers between devices, body(): lax.psum((weight_part, loss_portion), ('dp', 'mp'))  253 us
    psum x3, blocking collectives, prototype_totals(): return lax.psum(jnp.sum(values, axis=0), 'dp')  206 us
    psum x1, waiting for transfers between devices, body(): proto_grad = lax.psum(proto_grad, 'dp')  84 us
    psum x1, blocking collectives, body(): lax.psum((weight_part, loss_portion), ('dp', 'mp'))  80 us
    psum x3, blocking collectives, code_totals(): return lax.psum(jnp.sum(values, axis=-1), 'mp')  63.2 us
    all_gather x1, waiting for transfers between devices, body(): all_embed = lax.all_gather(embed_half, 'mp', axis=0, tiled=True)  46.3 us
  transfers between devices with their start and end apart: 4, of which 3 were waited for; matrix products, arithmetic and copies ran while one was open for 1% of the time, Pallas kernels for 0%

commit v1 on v0

v1 whole, which is shorter than its diff:
```python
import functools

import jax
import jax.numpy as jnp
from jax import lax
from jax.experimental import pallas as pl
from jax.experimental.pallas import tpu as pltpu
from jax.sharding import PartitionSpec as P

MESH = pl.DeviceIdType.MESH
BF = jnp.bfloat16
F32 = jnp.float32

EPSILON_CODES = 0.05
SOFTMAX_TEMPER = 0.1
LOSS_FACTOR = 4096.0
TINY = 1e-06

NX, NY, NC, NZ = 4, 4, 2, 8
NP = NX * NY
KS = 375
KP = 384
LT = KP // 128
NT = NZ * LT
WR = 256
D = 256
E = 512
HALF = KP // 2
RH = D // 2
PR_ROWS = RH // NP
GR = E // 2 // NP
GRP = GR + 8
XY = [(dx, dy) for dx in range(NX) for dy in range(NY) if dx or dy]
ZO = [1, 7, 2, 6, 3, 5, 4]


def nt_dot(a, b):
    return lax.dot_general(a, b, (((1,), (1,)), ((), ())), preferred_element_type=F32)


def dot(a, b):
    return jnp.dot(a, b, preferred_element_type=F32)


def kernel(
    batch_rows,
    feats, weight, protos,
    gproto_out, gweight_out, loss_out,
    pu, ph, unit, inv, emb, embt, xt,
    ex, sc, so, den, acc, vec, csum, cothers, gm,
    buf_a, buf_b, vec_b,
    eg, pg, buf_p, pr, buf_q, pq, buf_z, fg, gw, buf_w, gwr, buf_x, buf_y, fw, loss_acc,
    s_z, r_z, s_f, r_f, s_e, r_e, s_a, r_a, s_b, r_b, s_c, r_c,
    s_p, r_p, s_q, r_q, s_qz, r_qz, s_qg, r_qg, s_qc, r_qc,
    s_w, r_w, s_wx, r_wx, s_wz, r_wz, s_wg, r_wg, s_wc, r_wc,
):
    dp = lax.axis_index("dp")
    z = lax.axis_index("mp")
    x, y, c = dp // (NY * NC), (dp // NC) % NY, dp % NC
    o = 1 - c
    me_p = x * NY + y
    gf = LOSS_FACTOR / (2.0 * batch_rows * SOFTMAX_TEMPER)
    pending = []

    def plane(dx, dy):
        px, py = (x + dx) % NX, (y + dy) % NY
        return px * NY + py

    def plane_dev(p):
        return {"dp": p * NC + c, "mp": z}

    def z_dev(dz):
        return {"dp": dp, "mp": (z + dz) % NZ}

    sibling = {"dp": dp + 1 - 2 * c, "mp": z}

    def send(src, dst, ssem, rsem, device):
        copy = pltpu.make_async_remote_copy(
            src_ref=src, dst_ref=dst, send_sem=ssem, recv_sem=rsem, device_id=device, device_id_type=MESH
        )
        copy.start()
        pending.append(copy)
        return copy

    barrier = pltpu.get_barrier_semaphore()
    pl.semaphore_signal(barrier, inc=1, device_id=sibling, device_id_type=MESH)
    for dx, dy in XY:
        pl.semaphore_signal(barrier, inc=1, device_id=plane_dev(plane(dx, dy)), device_id_type=MESH)
    for dz in ZO:
        pl.semaphore_signal(barrier, inc=1, device_id=z_dev(dz), device_id_type=MESH)

    pu[...] = jnp.zeros_like(pu)
    own = protos[...]
    pu[0:KS, :] = own * lax.rsqrt(jnp.sum(own * own, axis=-1, keepdims=True) + TINY)
    ph[z] = pu[...].astype(BF)
    pl.semaphore_wait(barrier, 1 + len(XY) + len(ZO))

    zcopies = {}
    for i, dz in enumerate(ZO):
        part = ph.at[z, pl.ds(pl.multiple_of(c * HALF, HALF), HALF)]
        zcopies[dz] = send(part, part, s_z.at[i], r_z.at[i], z_dev(dz))

    def embed(view, row, erow):
        raw = dot(feats[view], weight[...])
        inverse = lax.rsqrt(jnp.sum(raw * raw, axis=-1, keepdims=True) + TINY)
        u = raw * inverse
        inv[row : row + WR, :] = inverse
        unit[row : row + WR, :] = u
        emb[erow : erow + WR, :] = u.astype(BF)

    embed(o, WR, 2 * WR)
    ecopy = send(emb.at[pl.ds(2 * WR, WR)], emb.at[pl.ds(WR, WR)], s_e, r_e, sibling)
    embed(c, 0, 0)
    ecopy.wait_recv()

    def scores_slab(q):
        pq_ = ph[q]
        tot = jnp.zeros((8, KP), F32)
        for b in range(2):
            s = nt_dot(emb[b * WR : (b + 1) * WR, :], pq_)
            e = jnp.exp(s * (1.0 / EPSILON_CODES))
            ex[q, b * WR : (b + 1) * WR, :] = e
            if b == 0:
                sc[q, 0:WR, :] = s
            tot = tot + jnp.sum(e.reshape(WR // 8, 8, KP), axis=0)
        acc[q] = tot

    scores_slab(z)
    for i, dz in enumerate(ZO):
        q = (z + NZ - dz) % NZ
        zcopies[dz].wait_recv()
        part = ph.at[q, pl.ds(pl.multiple_of(c * HALF, HALF), HALF)]
        fwd = send(part, part, s_f.at[i], r_f.at[i], sibling)
        fwd.wait_recv()
        scores_slab(q)

    lane = lax.broadcasted_iota(jnp.int32, (NT, 128), 1)
    row = lax.broadcasted_iota(jnp.int32, (NT, 128), 0)
    valid = lane + (row % LT) * 128 < KS

    def finish_column_sums(k):
        for q in range(NZ):
            part = jnp.sum(acc[q], axis=0, keepdims=True)
            for j in range(LT):
                vec[k, q * LT + j : q * LT + j + 1, :] = part[:, j * 128 : (j + 1) * 128]

    def reduce_columns(k, work_a, work_b):
        finish_column_sums(k)
        copies = []
        for i, (dx, dy) in enumerate(XY):
            copies.append(
                send(vec.at[k], buf_a.at[k, i], s_a.at[k, i], r_a.at[k, i], plane_dev(plane(dx, dy)))
            )
        work_a()
        total = vec[k]
        for i, copy in enumerate(copies):
            copy.wait_recv()
            total = total + buf_a[k, i]
        vec_b[k] = total
        copies = []
        for i, dz in enumerate(ZO):
            copies.append(send(vec_b.at[k], buf_b.at[k, i], s_b.at[k, i], r_b.at[k, i], z_dev(dz)))
        work_b()
        for i, copy in enumerate(copies):
            copy.wait_recv()
            total = total + buf_b[k, i]
        csum[k] = jnp.where(valid, 1.0 / total, 0.0)

    def other_view():
        def step(q, carry):
            s = nt_dot(emb[2 * WR : 3 * WR, :], ph[q])
            ex[q, 2 * WR : 3 * WR, :] = jnp.exp(s * (1.0 / EPSILON_CODES))
            sc[q, WR : 2 * WR, :] = s
            return carry

        lax.fori_loop(0, NZ, step, 0)

    last = lax.broadcasted_iota(jnp.int32, (1, 128), 1) < KS - (LT - 1) * 128

    def denominators(first):
        R = 64

        def step(b, carry):
            rows = pl.ds(pl.multiple_of(first + b * R, R), R)
            total = jnp.zeros((R, 128), F32)
            for q in range(NZ):
                s = jnp.exp(sc[q, rows, :] * (1.0 / SOFTMAX_TEMPER))
                so[q, rows, :] = s
                for j in range(LT):
                    part = s[:, j * 128 : (j + 1) * 128]
                    if j == LT - 1:
                        part = jnp.where(last, part, 0.0)
                    total = total + part
            den[rows, :] = jnp.sum(total, axis=1, keepdims=True)
            return carry

        lax.fori_loop(0, WR // R, step, 0)

    def transposes():
        embt[:, 0:WR] = emb[0:WR, :].astype(F32).T.astype(BF)
        embt[:, WR : 2 * WR] = emb[2 * WR : 3 * WR, :].astype(F32).T.astype(BF)

    def transposes_x():
        xt[:, 0:WR] = feats[c].astype(F32).T.astype(BF)
        xt[:, WR : 2 * WR] = feats[o].astype(F32).T.astype(BF)

    def row_inverse(cs, rows, R):
        total = jnp.zeros((R, 128), F32)
        for q in range(NZ):
            for j in range(LT):
                t = q * LT + j
                total = total + ex[q, rows, j * 128 : (j + 1) * 128] * cs[t : t + 1, :]
        return 1.0 / jnp.sum(total, axis=1, keepdims=True)

    def sinkhorn_pass(k):
        R = 64
        acc[...] = jnp.zeros_like(acc)

        def step(b, carry):
            rows = pl.ds(pl.multiple_of(b * R, R), R)
            r = row_inverse(csum.at[k], rows, R)
            for q in range(NZ):
                t = ex[q, rows, :] * r
                acc[q] += jnp.sum(t.reshape(R // 8, 8, KP), axis=0)
            return carry

        lax.fori_loop(0, 2 * WR // R, step, 0)

    def nothing():
        pass

    reduce_columns(0, other_view, lambda: denominators(0))
    sinkhorn_pass(0)
    reduce_columns(1, lambda: denominators(WR), transposes)
    sinkhorn_pass(1)
    reduce_columns(2, transposes_x, nothing)
    ccopy = send(csum.at[2], cothers, s_c, r_c, sibling)
    ccopy.wait_recv()

    RG = 32
    loss_acc[...] = jnp.zeros_like(loss_acc)

    def grad_step(b, carry):
        rows_c = pl.ds(pl.multiple_of(b * RG, RG), RG)
        rows_o = pl.ds(pl.multiple_of(WR + b * RG, RG), RG)
        erows_o = pl.ds(pl.multiple_of(2 * WR + b * RG, RG), RG)
        rc = row_inverse(csum.at[2], rows_c, RG) * gf
        ro = row_inverse(cothers, erows_o, RG) * gf
        dc = gf / den[rows_c, :]
        do = gf / den[rows_o, :]
        total = jnp.zeros((RG, 128), F32)
        for q in range(NZ):
            for j in range(LT):
                t = q * LT + j
                cols = slice(j * 128, (j + 1) * 128)
                ac = ex[q, rows_c, cols] * csum[2, t : t + 1, :] * rc
                ao = ex[q, erows_o, cols] * cothers[t : t + 1, :] * ro
                gm[q, rows_c, cols] = (so[q, rows_c, cols] * dc - ao).astype(BF)
                gm[q, rows_o, cols] = (so[q, rows_o, cols] * do - ac).astype(BF)
                total = total + ao * sc[q, rows_c, cols] + ac * sc[q, rows_o, cols]
        loss_acc[...] += jnp.sum(total.reshape(RG // 8, 8, 128), axis=0)
        return carry

    lax.fori_loop(0, WR // RG, grad_step, 0)

    eg[...] = jnp.zeros_like(eg)
    pcopies = []
    for q in range(NZ):
        pg[q] = dot(embt[...], gm[q])
        pcopies.append(
            send(pg.at[q, pl.ds(pl.multiple_of(o * RH, RH), RH)], buf_p.at[q], s_p.at[q], r_p.at[q], sibling)
        )
    for q in range(NZ):
        pcopies[q].wait_recv()
        pr[q] = pg[q, pl.ds(pl.multiple_of(c * RH, RH), RH), :] + buf_p[q]
    qcopies = []
    for i, (dx, dy) in enumerate(XY):
        p = plane(dx, dy)
        qcopies.append(
            send(
                pr.at[:, pl.ds(pl.multiple_of(p * PR_ROWS, PR_ROWS), PR_ROWS)],
                buf_q.at[i], s_q.at[i], r_q.at[i], plane_dev(p),
            )
        )

    for q in range(NZ):
        eg[...] += dot(gm[q], ph[q])
    along = jnp.sum(unit[...] * eg[...], axis=-1, keepdims=True)
    graw = ((eg[...] - unit[...] * along) * inv[...]).astype(BF)
    gfull = dot(xt[...], graw)
    for h in range(NC):
        for p in range(NP):
            first = h * (E // 2) + p * GR
            gw[h, p, 0:GR, :] = gfull[first : first + GR, :]
            gw[h, p, GR:GRP, :] = jnp.zeros((GRP - GR, D), F32)
    log_total = jnp.sum(jnp.log(den[...]))
    soft_total = jnp.sum(loss_acc[...]) * (1.0 / (SOFTMAX_TEMPER * gf))
    gw[0, 0, GR:GRP, :] = jnp.full((GRP - GR, D), soft_total - log_total, F32)
    wcopy = send(gw.at[o], buf_w, s_w, r_w, sibling)
    wcopy.wait_recv()
    gwr[...] = gw[c] + buf_w[...]
    wcopies = []
    for i, (dx, dy) in enumerate(XY):
        p = plane(dx, dy)
        wcopies.append(send(gwr.at[p], buf_x.at[i], s_wx.at[i], r_wx.at[i], plane_dev(p)))

    total = pr[:, pl.ds(pl.multiple_of(me_p * PR_ROWS, PR_ROWS), PR_ROWS), :]
    for i, copy in enumerate(qcopies):
        copy.wait_recv()
        total = total + buf_q[i]
    pq[...] = total
    zc = []
    for i, dz in enumerate(ZO):
        q = (z + dz) % NZ
        zc.append(send(pq.at[q], buf_z.at[i], s_qz.at[i], r_qz.at[i], z_dev(dz)))

    total = gwr[me_p]
    for i, copy in enumerate(wcopies):
        copy.wait_recv()
        total = total + buf_x[i]
    buf_y[z] = total
    wz = []
    for i, dz in enumerate(ZO):
        wz.append(send(buf_y.at[z], buf_y.at[z], s_wz.at[i], r_wz.at[i], z_dev(dz)))

    total = pq[z]
    for i, copy in enumerate(zc):
        copy.wait_recv()
        total = total + buf_z[i]
    fg[c, me_p] = total
    qg = []
    for i, (dx, dy) in enumerate(XY):
        qg.append(
            send(fg.at[c, me_p], fg.at[c, me_p], s_qg.at[i], r_qg.at[i], plane_dev(plane(dx, dy)))
        )

    for copy in wz:
        copy.wait_recv()
    total = buf_y[0]
    for k in range(1, NZ):
        total = total + buf_y[k]
    fw[c, me_p] = total
    wg = []
    for i, (dx, dy) in enumerate(XY):
        wg.append(
            send(fw.at[c, me_p], fw.at[c, me_p], s_wg.at[i], r_wg.at[i], plane_dev(plane(dx, dy)))
        )

    for copy in qg:
        copy.wait_recv()
    qc = send(fg.at[c], fg.at[c], s_qc, r_qc, sibling)
    qc.wait_recv()
    g = fg[...].reshape(D, KP).T
    u = pu[...]
    along_p = jnp.sum(u * g, axis=-1, keepdims=True)
    own = protos[...]
    pinv = lax.rsqrt(jnp.sum(own * own, axis=-1, keepdims=True) + TINY)
    gproto_out[...] = (g - u * along_p)[0:KS, :] * pinv

    for copy in wg:
        copy.wait_recv()
    wc = send(fw.at[c], fw.at[c], s_wc, r_wc, sibling)
    wc.wait_recv()
    for h in range(NC):
        for p in range(NP):
            first = h * (E // 2) + p * GR
            gweight_out[first : first + GR, :] = fw[h, p, 0:GR, :]
    loss_out[...] = fw[0, 0, GR:GRP, 0:128] * (-1.0 / (2.0 * batch_rows))

    for copy in pending:
        copy.wait_send()


def body(features, projection, prototypes):
    rows = features.shape[0]
    batch_rows = rows * lax.axis_size("dp")
    first = lax.axis_index("mp") * WR
    feats = lax.dynamic_slice_in_dim(features, first, WR, 0).transpose(1, 0, 2)
    dma = pltpu.SemaphoreType.DMA
    nxy, nz = len(XY), len(ZO)
    vm = pltpu.VMEM
    scratch = [
        vm((KP, D), F32), vm((NZ, KP, D), BF), vm((2 * WR, D), F32), vm((2 * WR, 1), F32),
        vm((3 * WR, D), BF), vm((D, 2 * WR), BF), vm((E, 2 * WR), BF),
        vm((NZ, 3 * WR, KP), F32), vm((NZ, 2 * WR, KP), F32), vm((NZ, 2 * WR, KP), F32),
        vm((2 * WR, 1), F32), vm((NZ, 8, KP), F32), vm((3, NT, 128), F32), vm((3, NT, 128), F32),
        vm((NT, 128), F32), vm((NZ, 2 * WR, KP), BF),
        vm((3, nxy, NT, 128), F32), vm((3, nz, NT, 128), F32), vm((3, NT, 128), F32),
        vm((2 * WR, D), F32), vm((NZ, D, KP), F32), vm((NZ, RH, KP), F32), vm((NZ, RH, KP), F32),
        vm((nxy, NZ, PR_ROWS, KP), F32), vm((NZ, PR_ROWS, KP), F32), vm((nz, PR_ROWS, KP), F32),
        vm((NC, NP, PR_ROWS, KP), F32), vm((NC, NP, GRP, D), F32), vm((NP, GRP, D), F32),
        vm((NP, GRP, D), F32), vm((nxy, GRP, D), F32), vm((NZ, GRP, D), F32), vm((NC, NP, GRP, D), F32),
        vm((8, 128), F32),
        dma((nz,)), dma((nz,)), dma((nz,)), dma((nz,)), dma, dma,
        dma((3, nxy)), dma((3, nxy)), dma((3, nz)), dma((3, nz)), dma, dma,
        dma((NZ,)), dma((NZ,)), dma((nxy,)), dma((nxy,)), dma((nz,)), dma((nz,)),
        dma((nxy,)), dma((nxy,)), dma, dma,
        dma, dma, dma((nxy,)), dma((nxy,)), dma((nz,)), dma((nz,)), dma((nxy,)), dma((nxy,)), dma, dma,
    ]
    vspec = pl.BlockSpec(memory_space=pltpu.VMEM)
    gproto, gweight, loss = pl.pallas_call(
        functools.partial(kernel, batch_rows),
        out_shape=(
            jax.ShapeDtypeStruct((KS, D), F32),
            jax.ShapeDtypeStruct((E, D), F32),
            jax.ShapeDtypeStruct((8, 128), F32),
        ),
        in_specs=[vspec] * 3,
        out_specs=(vspec,) * 3,
        scratch_shapes=scratch,
        compiler_params=pltpu.CompilerParams(
            collective_id=0, has_side_effects=True, vmem_limit_bytes=60 * 1024 * 1024
        ),
        name="swav",
    )(feats, projection, prototypes)
    return gproto, gweight, loss[0, 0]


def solution(mesh):
    return jax.shard_map(
        body,
        mesh=mesh,
        in_specs=(P("dp", None, None), P(), P("mp", None)),
        out_specs=(P("mp", None), P(), P()),
        check_vma=False,
    )
```

time: 804 us -> 131 us (0.16)
  waiting for transfers between devices: 383 us -> 0 us
  blocking collectives: 349 us -> 0 us
  Pallas kernels: 0 us -> 123 us
  other arithmetic: 32.9 us -> 0 us
  matrix products: 16 us -> 0 us
  between operations: 15.7 us -> 0.65 us
    psum x7 -> x0, blocking collectives: 349 us -> none  [the longest x3 206 us: prototype_totals(): return lax.psum(jnp.sum(values, axis=0), 'dp')]
    psum x2 -> x0, waiting for transfers between devices: 337 us -> none  [the longest x1 253 us: body(): lax.psum((weight_part, loss_portion), ('dp', 'mp'))]
    pallas_call x0 -> x1, Pallas kernels: none -> 123 us  [body(): pl.pallas_call(functools.partial(kernel, batch_rows), out_shape=(jax.Shap...]
    all_gather x1 -> x0, waiting for transfers between devices: 46.3 us -> none  [body(): all_embed = lax.all_gather(embed_half, 'mp', axis=0, tiled=True)]
    reduce_sum x8 -> x0, other arithmetic: 25.2 us -> none  [the longest x2 8.34 us: prototype_totals(): return lax.psum(jnp.sum(values, axis=0), 'dp')]
    dot_general x5 -> x0, matrix products: 16 us -> none  [the longest x1 5.43 us: body(): jnp.einsum('bvp,kp->bvk', all_embed, proto_half, preferred_element_type=j...]
  transfers between devices with their start and end apart: 4 -> 0, of which waited for: 3 -> 0; matrix products, arithmetic and copies ran while one was open for 1% -> 0% of each run, Pallas kernels for 0% -> 0%
where the time goes in v1:
time: 131 us
  Pallas kernels  123 us (94%)
  local copies, waits for them, and re-layouts  7.07 us (5%)
    pallas_call x1, Pallas kernels, body(): pl.pallas_call(functools.partial(kernel, batch_rows), out_shape=(jax.Shap...  123 us
    unnamed x3, local copies, waits for them, and re-layouts  4.47 us

profile of v1, /device:TPU:1, one launch (start us, length us, event | category | flops | bytes accessed | tf_op | source)
XLA Modules:
  0.0 130.5 jit_solution(5173915668393060430)
XLA Ops:
  0.6 1.4 %constant_dynamic-slice_fusion = bf16[256,2,512]{2,1,0:T(2,128)(2,1)S(1)} fusion(bf16[2048,2,512]{2,1,0:T(2,128)(2,1)} %param.3, s32[]{:T(128)S(6)} %select_n.3), kind=kLoop, calls=%fused_computation.1 | loop fusion | bytes 1048580 | tf_op jit(solution)/shard_map/dynamic_slice | solution.py:378
  2.0 0.8 copy.9
  2.9 122.8 %swav.1 = (f32[375,256]{1,0:T(8,128)}, f32[512,256]{1,0:T(8,128)}, f32[8,128]{1,0:T(8,128)}) custom-call(bf16[2,256,512]{2,1,0:T(8,128)(2,1)} %bitcast.4, bf16[512,256]{1,0:T(8,128)(2,1)} %weight.1, f32[375,256]{1,0:T(8,128)} %protos.1), custom_call_target="tpu_custom_call" | custom-call | tf_op jit(solution)/shard_map/swav/pallas_call | solution.py:401
  125.7 1.2 slice.3
  126.9 1.8 %copy.12 = f32[375,256]{1,0:T(8,128)} copy(f32[375,256]{1,0:T(8,128)} %get-tuple-element.12) | data formatting | bytes 768000
  128.6 1.9 %copy.13 = f32[512,256]{1,0:T(8,128)} copy(f32[512,256]{1,0:T(8,128)} %get-tuple-element.13) | data formatting | bytes 1048576

commit v2 on v1

--- a/solution.py
+++ b/solution.py
@@ -14,6 +14,7 @@
 EPSILON_CODES = 0.05
 SOFTMAX_TEMPER = 0.1
 LOSS_FACTOR = 4096.0
+VLIM = 60
 TINY = 1e-06
 
 NX, NY, NC, NZ = 4, 4, 2, 8
@@ -29,7 +30,10 @@
 RH = D // 2
 PR_ROWS = RH // NP
 GR = E // 2 // NP
-GRP = GR + 8
+GH = E // 2
+XL = 256
+GRPS = 4
+ORD = [4, 3, 5, 2, 6, 1, 7, 0]
 XY = [(dx, dy) for dx in range(NX) for dy in range(NY) if dx or dy]
 ZO = [1, 7, 2, 6, 3, 5, 4]
 
@@ -44,14 +48,15 @@
 
 def kernel(
     batch_rows,
-    feats, weight, protos,
-    gproto_out, gweight_out, loss_out,
+    feats_in, weight_in, protos_in,
+    gproto_out, gweight_out,
+    raw, feats, weight, protos, s_in,
     pu, ph, unit, inv, emb, embt, xt,
     ex, sc, so, den, acc, vec, csum, cothers, gm,
     buf_a, buf_b, vec_b,
-    eg, pg, buf_p, pr, buf_q, pq, buf_z, fg, gw, buf_w, gwr, buf_x, buf_y, fw, loss_acc,
+    eg, pg, buf_p, pr, buf_q, pq, buf_z, buf_f, zs, buf_xz, fg, gw, buf_w, gwr, buf_x, buf_y, fw, loss_acc,
     s_z, r_z, s_f, r_f, s_e, r_e, s_a, r_a, s_b, r_b, s_c, r_c,
-    s_p, r_p, s_q, r_q, s_qz, r_qz, s_qg, r_qg, s_qc, r_qc,
+    s_p, r_p, s_q, r_q, s_zf, r_zf, s_xz, r_xz, s_qz, r_qz, s_qg, r_qg, s_qc, r_qc,
     s_w, r_w, s_wx, r_wx, s_wz, r_wz, s_wg, r_wg, s_wc, r_wc,
 ):
     dp = lax.axis_index("dp")
@@ -82,6 +87,19 @@
         pending.append(copy)
         return copy
 
+    def arrival(dst, ssem, rsem):
+        return pltpu.make_async_remote_copy(
+            src_ref=dst, dst_ref=dst, send_sem=ssem, recv_sem=rsem, device_id=sibling, device_id_type=MESH
+        )
+
+    def zf_recv(dz):
+        k = (z + dz) % NZ
+        return arrival(buf_f.at[k], s_zf.at[0], r_zf.at[k])
+
+    def wz_recv(dz):
+        k = (z + dz) % NZ
+        return arrival(buf_y.at[k], s_wz.at[0], r_wz.at[k])
+
     barrier = pltpu.get_barrier_semaphore()
     pl.semaphore_signal(barrier, inc=1, device_id=sibling, device_id_type=MESH)
     for dx, dy in XY:
@@ -89,6 +107,15 @@
     for dz in ZO:
         pl.semaphore_signal(barrier, inc=1, device_id=z_dev(dz), device_id_type=MESH)
 
+    loads = [
+        pltpu.make_async_copy(protos_in, protos, s_in.at[0]),
+        pltpu.make_async_copy(feats_in.at[pl.ds(z * WR, WR)], raw, s_in.at[1]),
+        pltpu.make_async_copy(weight_in, weight, s_in.at[2]),
+    ]
+    for load in loads:
+        load.start()
+
+    loads[0].wait()
     pu[...] = jnp.zeros_like(pu)
     own = protos[...]
     pu[0:KS, :] = own * lax.rsqrt(jnp.sum(own * own, axis=-1, keepdims=True) + TINY)
@@ -99,6 +126,13 @@
     for i, dz in enumerate(ZO):
         part = ph.at[z, pl.ds(pl.multiple_of(c * HALF, HALF), HALF)]
         zcopies[dz] = send(part, part, s_z.at[i], r_z.at[i], z_dev(dz))
+
+    loads[1].wait()
+    loads[2].wait()
+    to = lax.broadcasted_iota(jnp.int32, (2 * WR, 2 * WR), 0)
+    fro = lax.broadcasted_iota(jnp.int32, (2 * WR, 2 * WR), 1)
+    order = ((to % WR) * 2 + to // WR == fro).astype(F32).astype(BF)
+    feats[...] = dot(order, raw[...].reshape(2 * WR, E)).astype(BF).reshape(2, WR, E)
 
     def embed(view, row, erow):
         raw = dot(feats[view], weight[...])
@@ -263,123 +297,160 @@
 
     lax.fori_loop(0, WR // RG, grad_step, 0)
 
+    log_total = jnp.sum(jnp.log(den[...]))
+    share = jnp.sum(loss_acc[...]) * (1.0 / (SOFTMAX_TEMPER * gf)) - log_total
+    spare = lax.broadcasted_iota(jnp.int32, (8, 128), 1) == 127
+
+    pcopies = []
+    for i, dz in enumerate(ORD):
+        q = (z + dz) % NZ
+        pg[i] = dot(embt[...], gm[q])
+        pg[i, 0:8, KP - 128 : KP] = jnp.where(spare, share, pg[i, 0:8, KP - 128 : KP])
+        pcopies.append(
+            send(pg.at[i, pl.ds(pl.multiple_of(o * RH, RH), RH)], buf_p.at[i], s_p.at[i], r_p.at[i], sibling)
+        )
     eg[...] = jnp.zeros_like(eg)
-    pcopies = []
-    for q in range(NZ):
-        pg[q] = dot(embt[...], gm[q])
-        pcopies.append(
-            send(pg.at[q, pl.ds(pl.multiple_of(o * RH, RH), RH)], buf_p.at[q], s_p.at[q], r_p.at[q], sibling)
-        )
-    for q in range(NZ):
-        pcopies[q].wait_recv()
-        pr[q] = pg[q, pl.ds(pl.multiple_of(c * RH, RH), RH), :] + buf_p[q]
     qcopies = []
-    for i, (dx, dy) in enumerate(XY):
-        p = plane(dx, dy)
-        qcopies.append(
-            send(
-                pr.at[:, pl.ds(pl.multiple_of(p * PR_ROWS, PR_ROWS), PR_ROWS)],
-                buf_q.at[i], s_q.at[i], r_q.at[i], plane_dev(p),
+    zf = []
+    for i, dz in enumerate(ORD):
+        q = (z + dz) % NZ
+        pcopies[i].wait_recv()
+        pr[i] = pg[i, pl.ds(pl.multiple_of(c * RH, RH), RH), :] + buf_p[i]
+        if dz:
+            zf.append(
+                send(pr.at[i, :, pl.ds(XL, KP - XL)], buf_f.at[z], s_zf.at[i], r_zf.at[z], z_dev(dz))
             )
-        )
-
-    for q in range(NZ):
+        else:
+            buf_f[z] = pr[i, :, XL:KP]
         eg[...] += dot(gm[q], ph[q])
+        if i % GRPS == GRPS - 1:
+            g = i // GRPS
+            for n, (dx, dy) in enumerate(XY):
+                p = plane(dx, dy)
+                qcopies.append(
+                    send(
+                        pr.at[pl.ds(g * GRPS, GRPS), pl.ds(pl.multiple_of(p * PR_ROWS, PR_ROWS), PR_ROWS), pl.ds(0, XL)],
+                        buf_q.at[n, pl.ds(g * GRPS, GRPS)], s_q.at[g, n], r_q.at[g, n], plane_dev(p),
+                    )
+                )
+
     along = jnp.sum(unit[...] * eg[...], axis=-1, keepdims=True)
     graw = ((eg[...] - unit[...] * along) * inv[...]).astype(BF)
-    gfull = dot(xt[...], graw)
-    for h in range(NC):
-        for p in range(NP):
-            first = h * (E // 2) + p * GR
-            gw[h, p, 0:GR, :] = gfull[first : first + GR, :]
-            gw[h, p, GR:GRP, :] = jnp.zeros((GRP - GR, D), F32)
-    log_total = jnp.sum(jnp.log(den[...]))
-    soft_total = jnp.sum(loss_acc[...]) * (1.0 / (SOFTMAX_TEMPER * gf))
-    gw[0, 0, GR:GRP, :] = jnp.full((GRP - GR, D), soft_total - log_total, F32)
-    wcopy = send(gw.at[o], buf_w, s_w, r_w, sibling)
+    gw[...] = dot(xt[...], graw)
+    wcopy = send(gw.at[pl.ds(pl.multiple_of(o * GH, GH), GH)], buf_w, s_w, r_w, sibling)
     wcopy.wait_recv()
-    gwr[...] = gw[c] + buf_w[...]
+    gwr[...] = gw[pl.ds(pl.multiple_of(c * GH, GH), GH), :] + buf_w[...]
     wcopies = []
     for i, (dx, dy) in enumerate(XY):
         p = plane(dx, dy)
-        wcopies.append(send(gwr.at[p], buf_x.at[i], s_wx.at[i], r_wx.at[i], plane_dev(p)))
-
-    total = pr[:, pl.ds(pl.multiple_of(me_p * PR_ROWS, PR_ROWS), PR_ROWS), :]
-    for i, copy in enumerate(qcopies):
-        copy.wait_recv()
-        total = total + buf_q[i]
-    pq[...] = total
-    zc = []
-    for i, dz in enumerate(ZO):
-        q = (z + dz) % NZ
-        zc.append(send(pq.at[q], buf_z.at[i], s_qz.at[i], r_qz.at[i], z_dev(dz)))
-
-    total = gwr[me_p]
+        wcopies.append(
+            send(gwr.at[pl.ds(pl.multiple_of(p * GR, GR), GR)], buf_x.at[i], s_wx.at[i], r_wx.at[i], plane_dev(p))
+        )
+
+    for i, dz in enumerate(ORD):
+        if dz:
+            zf_recv(dz).wait_recv()
+    total = buf_f[0]
+    for k in range(1, NZ):
+        total = total + buf_f[k]
+    zs[...] = total
+    xz = []
+    for i, (dx, dy) in enumerate(XY):
+        p = plane(dx, dy)
+        xz.append(
+            send(zs.at[pl.ds(pl.multiple_of(p * PR_ROWS, PR_ROWS), PR_ROWS)], buf_xz.at[i], s_xz.at[i], r_xz.at[i], plane_dev(p))
+        )
+
+    total = gwr[pl.ds(pl.multiple_of(me_p * GR, GR), GR), :]
     for i, copy in enumerate(wcopies):
         copy.wait_recv()
         total = total + buf_x[i]
     buf_y[z] = total
     wz = []
     for i, dz in enumerate(ZO):
-        wz.append(send(buf_y.at[z], buf_y.at[z], s_wz.at[i], r_wz.at[i], z_dev(dz)))
-
-    total = pq[z]
+        wz.append(send(buf_y.at[z], buf_y.at[z], s_wz.at[i], r_wz.at[z], z_dev(dz)))
+
+    total = pr[:, pl.ds(pl.multiple_of(me_p * PR_ROWS, PR_ROWS), PR_ROWS), 0:XL]
+    for copy in qcopies:
+        copy.wait_recv()
+    for n in range(len(XY)):
+        total = total + buf_q[n]
+    pq[...] = total
+    zc = []
+    for i, dz in enumerate(ORD):
+        if dz:
+            zc.append(send(pq.at[i], buf_z.at[i], s_qz.at[i], r_qz.at[i], z_dev(dz)))
+
+    total = zs[pl.ds(pl.multiple_of(me_p * PR_ROWS, PR_ROWS), PR_ROWS), :]
+    for i, copy in enumerate(xz):
+        copy.wait_recv()
+        total = total + buf_xz[i]
+    fg[c, me_p, :, XL:KP] = total
+    total = pq[NZ - 1]
     for i, copy in enumerate(zc):
         copy.wait_recv()
         total = total + buf_z[i]
-    fg[c, me_p] = total
+    fg[c, me_p, :, 0:XL] = total
     qg = []
     for i, (dx, dy) in enumerate(XY):
         qg.append(
-            send(fg.at[c, me_p], fg.at[c, me_p], s_qg.at[i], r_qg.at[i], plane_dev(plane(dx, dy)))
-        )
-
-    for copy in wz:
-        copy.wait_recv()
+            send(fg.at[c, me_p], fg.at[c, me_p], s_qg.at[i], r_qg.at[me_p], plane_dev(plane(dx, dy)))
+        )
+
+    for dz in ZO:
+        wz_recv(dz).wait_recv()
     total = buf_y[0]
     for k in range(1, NZ):
         total = total + buf_y[k]
-    fw[c, me_p] = total
+    mine = pl.ds(pl.multiple_of(c * GH + me_p * GR, GR), GR)
+    fw[mine, :] = total
     wg = []
     for i, (dx, dy) in enumerate(XY):
         wg.append(
-            send(fw.at[c, me_p], fw.at[c, me_p], s_wg.at[i], r_wg.at[i], plane_dev(plane(dx, dy)))
-        )
-
-    for copy in qg:
-        copy.wait_recv()
+            send(fw.at[mine], fw.at[mine], s_wg.at[i], r_wg.at[me_p], plane_dev(plane(dx, dy)))
+        )
+
+    for dx, dy in XY:
+        p = plane(dx, dy)
+        arrival(fg.at[c, p], s_qg.at[0], r_qg.at[p]).wait_recv()
     qc = send(fg.at[c], fg.at[c], s_qc, r_qc, sibling)
     qc.wait_recv()
-    g = fg[...].reshape(D, KP).T
-    u = pu[...]
-    along_p = jnp.sum(u * g, axis=-1, keepdims=True)
+    for dx, dy in XY:
+        p = plane(dx, dy)
+        arrival(fw.at[pl.ds(pl.multiple_of(c * GH + p * GR, GR), GR)], s_wg.at[0], r_wg.at[p]).wait_recv()
+    half = pl.ds(pl.multiple_of(c * GH, GH), GH)
+    wc = send(fw.at[half], fw.at[half], s_wc, r_wc, sibling)
+    wc.wait_recv()
+    out_f = pltpu.make_async_copy(fg, gproto_out, s_in.at[0])
+    out_w = pltpu.make_async_copy(fw, gweight_out, s_in.at[1])
+    out_f.start()
+    out_w.start()
+    out_f.wait()
+    out_w.wait()
+
+    for copy in pending:
+        copy.wait_send()
+
+
+def finish(batch_rows, fg, fw, protos, gproto_out, gweight_out, loss_out):
+    g = fg[...].reshape(D, KP).T[0:KS, :]
     own = protos[...]
     pinv = lax.rsqrt(jnp.sum(own * own, axis=-1, keepdims=True) + TINY)
-    gproto_out[...] = (g - u * along_p)[0:KS, :] * pinv
-
-    for copy in wg:
-        copy.wait_recv()
-    wc = send(fw.at[c], fw.at[c], s_wc, r_wc, sibling)
-    wc.wait_recv()
-    for h in range(NC):
-        for p in range(NP):
-            first = h * (E // 2) + p * GR
-            gweight_out[first : first + GR, :] = fw[h, p, 0:GR, :]
-    loss_out[...] = fw[0, 0, GR:GRP, 0:128] * (-1.0 / (2.0 * batch_rows))
-
-    for copy in pending:
-        copy.wait_send()
+    u = own * pinv
+    along = jnp.sum(u * g, axis=-1, keepdims=True)
+    gproto_out[...] = (g - u * along) * pinv
+    gweight_out[...] = fw[...]
+    loss_out[...] = fg[0, 0, 0:1, KP - 1 : KP] * (-1.0 / (2.0 * batch_rows))
 
 
 def body(features, projection, prototypes):
     rows = features.shape[0]
     batch_rows = rows * lax.axis_size("dp")
-    first = lax.axis_index("mp") * WR
-    feats = lax.dynamic_slice_in_dim(features, first, WR, 0).transpose(1, 0, 2)
     dma = pltpu.SemaphoreType.DMA
     nxy, nz = len(XY), len(ZO)
     vm = pltpu.VMEM
     scratch = [
+        vm((WR, 2, E), BF), vm((2, WR, E), BF), vm((E, D), BF), vm((KS, D), F32), dma((3,)),
         vm((KP, D), F32), vm((NZ, KP, D), BF), vm((2 * WR, D), F32), vm((2 * WR, 1), F32),
         vm((3 * WR, D), BF), vm((D, 2 * WR), BF), vm((E, 2 * WR), BF),
         vm((NZ, 3 * WR, KP), F32), vm((NZ, 2 * WR, KP), F32), vm((NZ, 2 * WR, KP), F32),
@@ -387,33 +458,45 @@
         vm((NT, 128), F32), vm((NZ, 2 * WR, KP), BF),
         vm((3, nxy, NT, 128), F32), vm((3, nz, NT, 128), F32), vm((3, NT, 128), F32),
         vm((2 * WR, D), F32), vm((NZ, D, KP), F32), vm((NZ, RH, KP), F32), vm((NZ, RH, KP), F32),
-        vm((nxy, NZ, PR_ROWS, KP), F32), vm((NZ, PR_ROWS, KP), F32), vm((nz, PR_ROWS, KP), F32),
-        vm((NC, NP, PR_ROWS, KP), F32), vm((NC, NP, GRP, D), F32), vm((NP, GRP, D), F32),
-        vm((NP, GRP, D), F32), vm((nxy, GRP, D), F32), vm((NZ, GRP, D), F32), vm((NC, NP, GRP, D), F32),
+        vm((nxy, NZ, PR_ROWS, XL), F32), vm((NZ, PR_ROWS, XL), F32), vm((nz, PR_ROWS, XL), F32),
+        vm((NZ, RH, KP - XL), F32), vm((RH, KP - XL), F32), vm((nxy, PR_ROWS, KP - XL), F32),
+        vm((NC, NP, PR_ROWS, KP), F32), vm((E, D), F32), vm((GH, D), F32),
+        vm((GH, D), F32), vm((nxy, GR, D), F32), vm((NZ, GR, D), F32), vm((E, D), F32),
         vm((8, 128), F32),
         dma((nz,)), dma((nz,)), dma((nz,)), dma((nz,)), dma, dma,
         dma((3, nxy)), dma((3, nxy)), dma((3, nz)), dma((3, nz)), dma, dma,
-        dma((NZ,)), dma((NZ,)), dma((nxy,)), dma((nxy,)), dma((nz,)), dma((nz,)),
-        dma((nxy,)), dma((nxy,)), dma, dma,
-        dma, dma, dma((nxy,)), dma((nxy,)), dma((nz,)), dma((nz,)), dma((nxy,)), dma((nxy,)), dma, dma,
+        dma((NZ,)), dma((NZ,)), dma((NZ // GRPS, nxy)), dma((NZ // GRPS, nxy)), dma((NZ,)), dma((NZ,)),
+        dma((nxy,)), dma((nxy,)), dma((nz,)), dma((nz,)), dma((nxy,)), dma((NP,)), dma, dma,
+        dma, dma, dma((nxy,)), dma((nxy,)), dma((nz,)), dma((NZ,)), dma((nxy,)), dma((NP,)), dma, dma,
     ]
     vspec = pl.BlockSpec(memory_space=pltpu.VMEM)
+    aspec = pl.BlockSpec(memory_space=pl.ANY)
+    fg, fw = pl.pallas_call(
+        functools.partial(kernel, batch_rows),
+        out_shape=(
+            jax.ShapeDtypeStruct((NC, NP, PR_ROWS, KP), F32),
+            jax.ShapeDtypeStruct((E, D), F32),
+        ),
+        in_specs=[aspec] * 3,
+        out_specs=(aspec,) * 2,
+        scratch_shapes=scratch,
+        compiler_params=pltpu.CompilerParams(
+            collective_id=0, has_side_effects=True, vmem_limit_bytes=VLIM * 1024 * 1024
+        ),
+        name="swav",
+    )(features, projection, prototypes)
     gproto, gweight, loss = pl.pallas_call(
-        functools.partial(kernel, batch_rows),
+        functools.partial(finish, batch_rows),
         out_shape=(
             jax.ShapeDtypeStruct((KS, D), F32),
             jax.ShapeDtypeStruct((E, D), F32),
-            jax.ShapeDtypeStruct((8, 128), F32),
+            jax.ShapeDtypeStruct((1, 1), F32),
         ),
         in_specs=[vspec] * 3,
         out_specs=(vspec,) * 3,
-        scratch_shapes=scratch,
-        compiler_params=pltpu.CompilerParams(
-            collective_id=0, has_side_effects=True, vmem_limit_bytes=60 * 1024 * 1024
-        ),
-        name="swav",
-    )(feats, projection, prototypes)
-    return gproto, gweight, loss[0, 0]
+        name="finish",
+    )(fg, fw, prototypes)
+    return gproto, gweight, loss.reshape(())
 
 
 def solution(mesh):

time: 131 us -> 120 us (0.916)
  local copies, waits for them, and re-layouts: 7.07 us -> 0 us
  Pallas kernels: 123 us -> 119 us
    pallas_call x1, Pallas kernels: 123 us -> 117 us  [body(): pl.pallas_call(functools.partial(kernel, batch_rows), out_shape=(jax.Shap...]
    unnamed x3 -> x0, local copies, waits for them, and re-layouts: 4.47 us -> none
    pallas_call x0 -> x1, Pallas kernels: none -> 2.48 us  [body(): pl.pallas_call(functools.partial(finish, batch_rows), out_shape=(jax.Shap...]
    dynamic_slice x1 -> x0, local copies, waits for them, and re-layouts: 1.41 us -> none  [body(): feats = lax.dynamic_slice_in_dim(features, first, WR, 0).transpose(1, 0, 2)]
where the time goes in v2:
time: 120 us
  Pallas kernels  119 us (99%)
    pallas_call x1, Pallas kernels, body(): pl.pallas_call(functools.partial(kernel, batch_rows), out_shape=(jax.Shap...  117 us
    pallas_call x1, Pallas kernels, body(): pl.pallas_call(functools.partial(finish, batch_rows), out_shape=(jax.Shap...  2.48 us

profile of v2, /device:TPU:1, one launch (start us, length us, event | category | flops | bytes accessed | tf_op | source)
XLA Modules:
  0.0 120.0 jit_solution(9842683435440744533)
XLA Ops:
  0.6 116.9 %swav.1 = (f32[2,16,8,384]{3,2,1,0:T(8,128)}, f32[512,256]{1,0:T(8,128)}) custom-call(bf16[2048,2,512]{2,1,0:T(2,128)(2,1)} %feats_in.1, bf16[512,256]{1,0:T(8,128)(2,1)} %weight_in.1, f32[375,256]{1,0:T(8,128)} %protos.1), custom_call_target="tpu_custom_call" | custom-call | tf_op jit(solution)/shard_map/swav/pallas_call | solution.py:474
  117.5 2.5 %finish.1 = (f32[375,256]{1,0:T(8,128)}, f32[512,256]{1,0:T(8,128)}, f32[1,1]{1,0:T(1,128)}) custom-call(f32[2,16,8,384]{3,2,1,0:T(8,128)} %get-tuple-element.8.fg, f32[512,256]{1,0:T(8,128)} %get-tuple-element.9.fw, f32[375,256]{1,0:T(8,128)} %protos.1), custom_call_target="tpu_custom_call" | custom-call | tf_op jit(solution)/shard_map/finish/pallas_call | solution.py:488

commit v3 on v2

--- a/solution.py
+++ b/solution.py
@@ -27,13 +27,10 @@
 D = 256
 E = 512
 HALF = KP // 2
-RH = D // 2
-PR_ROWS = RH // NP
-GR = E // 2 // NP
+DH = D // 2
+PR_ROWS = KP // NP
 GH = E // 2
-XL = 256
-GRPS = 4
-ORD = [4, 3, 5, 2, 6, 1, 7, 0]
+GR = GH // NP
 XY = [(dx, dy) for dx in range(NX) for dy in range(NY) if dx or dy]
 ZO = [1, 7, 2, 6, 3, 5, 4]
 
@@ -51,12 +48,12 @@
     feats_in, weight_in, protos_in,
     gproto_out, gweight_out,
     raw, feats, weight, protos, s_in,
-    pu, ph, unit, inv, emb, embt, xt,
-    ex, sc, so, den, acc, vec, csum, cothers, gm,
+    pu, ph, unit, inv, emb, emb_line, xt,
+    ex, sc, so, so_line, den, rsc, acc, vec, csum, cothers, gm,
     buf_a, buf_b, vec_b,
-    eg, pg, buf_p, pr, buf_q, pq, buf_z, buf_f, zs, buf_xz, fg, gw, buf_w, gwr, buf_x, buf_y, fw, loss_acc,
+    eg, gm_line, col, lanes, share_z, pg, buf_p, pr, buf_q, fg, gw, buf_w, gwr, buf_x, buf_y, fw, loss_acc,
     s_z, r_z, s_f, r_f, s_e, r_e, s_a, r_a, s_b, r_b, s_c, r_c,
-    s_p, r_p, s_q, r_q, s_zf, r_zf, s_xz, r_xz, s_qz, r_qz, s_qg, r_qg, s_qc, r_qc,
+    s_l, r_l, s_v, r_v, s_h, r_h, s_p, r_p, s_q, r_q, s_qg, r_qg, s_qc, r_qc,
     s_w, r_w, s_wx, r_wx, s_wz, r_wz, s_wg, r_wg, s_wc, r_wc,
 ):
     dp = lax.axis_index("dp")
@@ -91,10 +88,6 @@
         return pltpu.make_async_remote_copy(
             src_ref=dst, dst_ref=dst, send_sem=ssem, recv_sem=rsem, device_id=sibling, device_id_type=MESH
         )
-
-    def zf_recv(dz):
-        k = (z + dz) % NZ
-        return arrival(buf_f.at[k], s_zf.at[0], r_zf.at[k])
 
     def wz_recv(dz):
         k = (z + dz) % NZ
@@ -230,9 +223,36 @@
 
         lax.fori_loop(0, WR // R, step, 0)
 
-    def transposes():
-        embt[:, 0:WR] = emb[0:WR, :].astype(F32).T.astype(BF)
-        embt[:, WR : 2 * WR] = emb[2 * WR : 3 * WR, :].astype(F32).T.astype(BF)
+    def line_slot(dz):
+        return (z + NZ + dz) % NZ
+
+    def line_step(n):
+        for i, way in enumerate((1, -1)):
+            slot = line_slot(-way * (n - 1))
+            part = emb_line.at[slot]
+            if n == NZ // 2:
+                part = emb_line.at[slot, pl.ds(i * WR, WR)]
+            send(part, part, s_l.at[n - 1, i], r_l.at[n - 1, i], z_dev(way % NZ))
+
+    def line_wait(n):
+        for i, way in enumerate((1, -1)):
+            slot = line_slot(-way * n)
+            part = emb_line.at[slot]
+            if n == NZ // 2:
+                part = emb_line.at[slot, pl.ds(i * WR, WR)]
+            arrival(part, s_l.at[n - 1, i], r_l.at[n - 1, i]).wait_recv()
+
+    def line_scores(dz):
+        slot = line_slot(dz)
+        s = nt_dot(ph[z], emb_line[slot])
+        so_line[slot] = jnp.exp(s * (1.0 / SOFTMAX_TEMPER))
+
+    eye = lax.broadcasted_iota(jnp.int32, (128, 128), 0) == lax.broadcasted_iota(jnp.int32, (128, 128), 1)
+
+    def to_lanes(ref, row):
+        for i in range(2 * WR // 128):
+            part = jnp.broadcast_to(ref[i * 128 : (i + 1) * 128, :], (128, 128))
+            lanes[z, row + i : row + i + 1, :] = jnp.sum(jnp.where(eye, part, 0.0), axis=0, keepdims=True)
 
     def transposes_x():
         xt[:, 0:WR] = feats[c].astype(F32).T.astype(BF)
@@ -263,13 +283,53 @@
     def nothing():
         pass
 
-    reduce_columns(0, other_view, lambda: denominators(0))
+    emb_line[z, 0:WR, :] = emb[0:WR, :]
+    emb_line[z, WR : 2 * WR, :] = emb[2 * WR : 3 * WR, :]
+
+    def work_1a():
+        line_step(1)
+        other_view()
+        line_scores(0)
+
+    def work_2b():
+        line_scores(-1)
+        line_scores(1)
+        to_lanes(den, 4)
+
+    def work_3a():
+        transposes_x()
+        line_scores(-2)
+
+    reduce_columns(0, work_1a, lambda: denominators(0))
+    line_wait(1)
+    line_step(2)
     sinkhorn_pass(0)
-    reduce_columns(1, lambda: denominators(WR), transposes)
+    reduce_columns(1, lambda: denominators(WR), work_2b)
+    line_wait(2)
+    line_step(3)
     sinkhorn_pass(1)
-    reduce_columns(2, transposes_x, nothing)
+    reduce_columns(2, work_3a, lambda: line_scores(2))
     ccopy = send(csum.at[2], cothers, s_c, r_c, sibling)
+    line_wait(3)
+    line_step(4)
+
+    def row_scales(cs, row, erow):
+        def step(b, carry):
+            R = 64
+            rows = pl.ds(pl.multiple_of(row + b * R, R), R)
+            rsc[rows, :] = row_inverse(cs, pl.ds(pl.multiple_of(erow + b * R, R), R), R)
+            return carry
+
+        lax.fori_loop(0, WR // 64, step, 0)
+
+    row_scales(csum.at[2], 0, 0)
     ccopy.wait_recv()
+    row_scales(cothers, WR, 2 * WR)
+    to_lanes(rsc, 0)
+    for i, dz in enumerate(ZO):
+        send(lanes.at[z], lanes.at[z], s_v.at[i], r_v.at[z], z_dev(dz))
+    line_scores(-3)
+    line_scores(3)
 
     RG = 32
     loss_acc[...] = jnp.zeros_like(loss_acc)
@@ -278,8 +338,8 @@
         rows_c = pl.ds(pl.multiple_of(b * RG, RG), RG)
         rows_o = pl.ds(pl.multiple_of(WR + b * RG, RG), RG)
         erows_o = pl.ds(pl.multiple_of(2 * WR + b * RG, RG), RG)
-        rc = row_inverse(csum.at[2], rows_c, RG) * gf
-        ro = row_inverse(cothers, erows_o, RG) * gf
+        rc = rsc[rows_c, :] * gf
+        ro = rsc[rows_o, :] * gf
         dc = gf / den[rows_c, :]
         do = gf / den[rows_o, :]
         total = jnp.zeros((RG, 128), F32)
@@ -299,41 +359,14 @@
 
     log_total = jnp.sum(jnp.log(den[...]))
     share = jnp.sum(loss_acc[...]) * (1.0 / (SOFTMAX_TEMPER * gf)) - log_total
-    spare = lax.broadcasted_iota(jnp.int32, (8, 128), 1) == 127
-
-    pcopies = []
-    for i, dz in enumerate(ORD):
-        q = (z + dz) % NZ
-        pg[i] = dot(embt[...], gm[q])
-        pg[i, 0:8, KP - 128 : KP] = jnp.where(spare, share, pg[i, 0:8, KP - 128 : KP])
-        pcopies.append(
-            send(pg.at[i, pl.ds(pl.multiple_of(o * RH, RH), RH)], buf_p.at[i], s_p.at[i], r_p.at[i], sibling)
-        )
-    eg[...] = jnp.zeros_like(eg)
-    qcopies = []
-    zf = []
-    for i, dz in enumerate(ORD):
-        q = (z + dz) % NZ
-        pcopies[i].wait_recv()
-        pr[i] = pg[i, pl.ds(pl.multiple_of(c * RH, RH), RH), :] + buf_p[i]
-        if dz:
-            zf.append(
-                send(pr.at[i, :, pl.ds(XL, KP - XL)], buf_f.at[z], s_zf.at[i], r_zf.at[z], z_dev(dz))
-            )
-        else:
-            buf_f[z] = pr[i, :, XL:KP]
-        eg[...] += dot(gm[q], ph[q])
-        if i % GRPS == GRPS - 1:
-            g = i // GRPS
-            for n, (dx, dy) in enumerate(XY):
-                p = plane(dx, dy)
-                qcopies.append(
-                    send(
-                        pr.at[pl.ds(g * GRPS, GRPS), pl.ds(pl.multiple_of(p * PR_ROWS, PR_ROWS), PR_ROWS), pl.ds(0, XL)],
-                        buf_q.at[n, pl.ds(g * GRPS, GRPS)], s_q.at[g, n], r_q.at[g, n], plane_dev(p),
-                    )
-                )
-
+    share_z[z] = jnp.full((8, 128), share, F32)
+    for i, dz in enumerate(ZO):
+        send(share_z.at[z], share_z.at[z], s_h.at[i], r_h.at[z], z_dev(dz))
+
+    grads = jnp.zeros((2 * WR, D), F32)
+    for q in range(NZ):
+        grads = grads + dot(gm[q], ph[q])
+    eg[...] = grads
     along = jnp.sum(unit[...] * eg[...], axis=-1, keepdims=True)
     graw = ((eg[...] - unit[...] * along) * inv[...]).astype(BF)
     gw[...] = dot(xt[...], graw)
@@ -347,18 +380,53 @@
             send(gwr.at[pl.ds(pl.multiple_of(p * GR, GR), GR)], buf_x.at[i], s_wx.at[i], r_wx.at[i], plane_dev(p))
         )
 
-    for i, dz in enumerate(ORD):
-        if dz:
-            zf_recv(dz).wait_recv()
-    total = buf_f[0]
+    for v, cs in enumerate((csum.at[2], cothers)):
+        for j in range(LT):
+            part = jnp.broadcast_to(cs[pl.ds(z * LT + j, 1), :], (128, 128))
+            part = jnp.sum(jnp.where(eye, part, 0.0), axis=1, keepdims=True)
+            col[v, j * 128 : (j + 1) * 128, :] = jnp.broadcast_to(part, (128, 128))
+    line_wait(4)
+    line_scores(4)
+    for dz in ZO:
+        k = line_slot(dz)
+        arrival(lanes.at[k], s_v.at[0], r_v.at[k]).wait_recv()
+
+    def line_grad(k, carry):
+        scale = [lanes[k, i : i + 1, :] * gf for i in range(4)]
+        soft = [gf / lanes[k, i : i + 1, :] for i in range(4, 8)]
+        R = 32
+        for b in range(KP // R):
+            rows = slice(b * R, (b + 1) * R)
+            for i in range(2):
+                lc, lo = slice(i * 128, (i + 1) * 128), slice(WR + i * 128, WR + (i + 1) * 128)
+                sc_, so_ = so_line[k, rows, lc], so_line[k, rows, lo]
+                ac = sc_ * sc_ * col[0, rows, :] * scale[i]
+                ao = so_ * so_ * col[1, rows, :] * scale[2 + i]
+                gm_line[k, rows, lc] = (sc_ * soft[i] - ao).astype(BF)
+                gm_line[k, rows, lo] = (so_ * soft[2 + i] - ac).astype(BF)
+        return carry
+
+    lax.fori_loop(0, NZ, line_grad, 0)
+    grads = jnp.zeros((KP, D), F32)
+    for k in range(NZ):
+        grads = grads + dot(gm_line[k], emb_line[k])
+    pg[...] = grads
+    for dz in ZO:
+        k = line_slot(dz)
+        arrival(share_z.at[k], s_h.at[0], r_h.at[k]).wait_recv()
+    share = share_z[0, 0:1, 0:1]
     for k in range(1, NZ):
-        total = total + buf_f[k]
-    zs[...] = total
-    xz = []
+        share = share + share_z[k, 0:1, 0:1]
+    spare = lax.broadcasted_iota(jnp.int32, (8, D), 0) == 7
+    pg[KP - 8 : KP, :] = jnp.where(spare, share, pg[KP - 8 : KP, :])
+    pcopy = send(pg.at[:, pl.ds(pl.multiple_of(o * DH, DH), DH)], buf_p, s_p, r_p, sibling)
+    pcopy.wait_recv()
+    pr[...] = pg[:, pl.ds(pl.multiple_of(c * DH, DH), DH)] + buf_p[...]
+    qcopies = []
     for i, (dx, dy) in enumerate(XY):
         p = plane(dx, dy)
-        xz.append(
-            send(zs.at[pl.ds(pl.multiple_of(p * PR_ROWS, PR_ROWS), PR_ROWS)], buf_xz.at[i], s_xz.at[i], r_xz.at[i], plane_dev(p))
+        qcopies.append(
+            send(pr.at[pl.ds(pl.multiple_of(p * PR_ROWS, PR_ROWS), PR_ROWS)], buf_q.at[i], s_q.at[i], r_q.at[i], plane_dev(p))
         )
 
     total = gwr[pl.ds(pl.multiple_of(me_p * GR, GR), GR), :]
@@ -370,32 +438,14 @@
     for i, dz in enumerate(ZO):
         wz.append(send(buf_y.at[z], buf_y.at[z], s_wz.at[i], r_wz.at[z], z_dev(dz)))
 
-    total = pr[:, pl.ds(pl.multiple_of(me_p * PR_ROWS, PR_ROWS), PR_ROWS), 0:XL]
-    for copy in qcopies:
+    mine = pl.ds(pl.multiple_of(me_p * PR_ROWS, PR_ROWS), PR_ROWS)
+    total = pr[mine, :]
+    for i, copy in enumerate(qcopies):
         copy.wait_recv()
-    for n in range(len(XY)):
-        total = total + buf_q[n]
-    pq[...] = total
-    zc = []
-    for i, dz in enumerate(ORD):
-        if dz:
-            zc.append(send(pq.at[i], buf_z.at[i], s_qz.at[i], r_qz.at[i], z_dev(dz)))
-
-    total = zs[pl.ds(pl.multiple_of(me_p * PR_ROWS, PR_ROWS), PR_ROWS), :]
-    for i, copy in enumerate(xz):
-        copy.wait_recv()
-        total = total + buf_xz[i]
-    fg[c, me_p, :, XL:KP] = total
-    total = pq[NZ - 1]
-    for i, copy in enumerate(zc):
-        copy.wait_recv()
-        total = total + buf_z[i]
-    fg[c, me_p, :, 0:XL] = total
-    qg = []
+        total = total + buf_q[i]
+    fg[c, mine, :] = total
     for i, (dx, dy) in enumerate(XY):
-        qg.append(
-            send(fg.at[c, me_p], fg.at[c, me_p], s_qg.at[i], r_qg.at[me_p], plane_dev(plane(dx, dy)))
-        )
+        send(fg.at[c, mine], fg.at[c, mine], s_qg.at[i], r_qg.at[me_p], plane_dev(plane(dx, dy)))
 
     for dz in ZO:
         wz_recv(dz).wait_recv()
@@ -412,7 +462,8 @@
 
     for dx, dy in XY:
         p = plane(dx, dy)
-        arrival(fg.at[c, p], s_qg.at[0], r_qg.at[p]).wait_recv()
+        part = pl.ds(pl.multiple_of(p * PR_ROWS, PR_ROWS), PR_ROWS)
+        arrival(fg.at[c, part], s_qg.at[0], r_qg.at[p]).wait_recv()
     qc = send(fg.at[c], fg.at[c], s_qc, r_qc, sibling)
     qc.wait_recv()
     for dx, dy in XY:
@@ -433,14 +484,14 @@
 
 
 def finish(batch_rows, fg, fw, protos, gproto_out, gweight_out, loss_out):
-    g = fg[...].reshape(D, KP).T[0:KS, :]
+    g = jnp.concatenate([fg[0], fg[1]], axis=1)[0:KS, :]
     own = protos[...]
     pinv = lax.rsqrt(jnp.sum(own * own, axis=-1, keepdims=True) + TINY)
     u = own * pinv
     along = jnp.sum(u * g, axis=-1, keepdims=True)
     gproto_out[...] = (g - u * along) * pinv
     gweight_out[...] = fw[...]
-    loss_out[...] = fg[0, 0, 0:1, KP - 1 : KP] * (-1.0 / (2.0 * batch_rows))
+    loss_out[...] = fg[0, KP - 1 : KP, 0:1] * (-1.0 / (2.0 * batch_rows))
 
 
 def body(features, projection, prototypes):
@@ -452,21 +503,19 @@
     scratch = [
         vm((WR, 2, E), BF), vm((2, WR, E), BF), vm((E, D), BF), vm((KS, D), F32), dma((3,)),
         vm((KP, D), F32), vm((NZ, KP, D), BF), vm((2 * WR, D), F32), vm((2 * WR, 1), F32),
-        vm((3 * WR, D), BF), vm((D, 2 * WR), BF), vm((E, 2 * WR), BF),
-        vm((NZ, 3 * WR, KP), F32), vm((NZ, 2 * WR, KP), F32), vm((NZ, 2 * WR, KP), F32),
-        vm((2 * WR, 1), F32), vm((NZ, 8, KP), F32), vm((3, NT, 128), F32), vm((3, NT, 128), F32),
+        vm((3 * WR, D), BF), vm((NZ, 2 * WR, D), BF), vm((E, 2 * WR), BF),
+        vm((NZ, 3 * WR, KP), F32), vm((NZ, 2 * WR, KP), F32), vm((NZ, 2 * WR, KP), F32), vm((NZ, KP, 2 * WR), F32),
+        vm((2 * WR, 1), F32), vm((2 * WR, 1), F32), vm((NZ, 8, KP), F32), vm((3, NT, 128), F32), vm((3, NT, 128), F32),
         vm((NT, 128), F32), vm((NZ, 2 * WR, KP), BF),
         vm((3, nxy, NT, 128), F32), vm((3, nz, NT, 128), F32), vm((3, NT, 128), F32),
-        vm((2 * WR, D), F32), vm((NZ, D, KP), F32), vm((NZ, RH, KP), F32), vm((NZ, RH, KP), F32),
-        vm((nxy, NZ, PR_ROWS, XL), F32), vm((NZ, PR_ROWS, XL), F32), vm((nz, PR_ROWS, XL), F32),
-        vm((NZ, RH, KP - XL), F32), vm((RH, KP - XL), F32), vm((nxy, PR_ROWS, KP - XL), F32),
-        vm((NC, NP, PR_ROWS, KP), F32), vm((E, D), F32), vm((GH, D), F32),
-        vm((GH, D), F32), vm((nxy, GR, D), F32), vm((NZ, GR, D), F32), vm((E, D), F32),
+        vm((2 * WR, D), F32), vm((NZ, KP, 2 * WR), BF), vm((2, KP, 128), F32), vm((NZ, 8, 128), F32), vm((NZ, 8, 128), F32),
+        vm((KP, D), F32), vm((KP, DH), F32), vm((KP, DH), F32), vm((nxy, PR_ROWS, DH), F32), vm((NC, KP, DH), F32),
+        vm((E, D), F32), vm((GH, D), F32), vm((GH, D), F32), vm((nxy, GR, D), F32), vm((NZ, GR, D), F32), vm((E, D), F32),
         vm((8, 128), F32),
         dma((nz,)), dma((nz,)), dma((nz,)), dma((nz,)), dma, dma,
         dma((3, nxy)), dma((3, nxy)), dma((3, nz)), dma((3, nz)), dma, dma,
-        dma((NZ,)), dma((NZ,)), dma((NZ // GRPS, nxy)), dma((NZ // GRPS, nxy)), dma((NZ,)), dma((NZ,)),
-        dma((nxy,)), dma((nxy,)), dma((nz,)), dma((nz,)), dma((nxy,)), dma((NP,)), dma, dma,
+        dma((4, 2)), dma((4, 2)), dma((nz,)), dma((NZ,)), dma((nz,)), dma((NZ,)), dma, dma,
+        dma((nxy,)), dma((nxy,)), dma((nxy,)), dma((NP,)), dma, dma,
         dma, dma, dma((nxy,)), dma((nxy,)), dma((nz,)), dma((NZ,)), dma((nxy,)), dma((NP,)), dma, dma,
     ]
     vspec = pl.BlockSpec(memory_space=pltpu.VMEM)
@@ -474,7 +523,7 @@
     fg, fw = pl.pallas_call(
         functools.partial(kernel, batch_rows),
         out_shape=(
-            jax.ShapeDtypeStruct((NC, NP, PR_ROWS, KP), F32),
+            jax.ShapeDtypeStruct((NC, KP, DH), F32),
             jax.ShapeDtypeStruct((E, D), F32),
         ),
         in_specs=[aspec] * 3,

time: 120 us -> 106 us (0.88)
  Pallas kernels: 119 us -> 105 us
    pallas_call x1, Pallas kernels: 117 us -> 103 us  [body(): pl.pallas_call(functools.partial(kernel, batch_rows), out_shape=(jax.Shap...]
where the time goes in v3:
time: 106 us
  Pallas kernels  105 us (99%)
    pallas_call x1, Pallas kernels, body(): pl.pallas_call(functools.partial(kernel, batch_rows), out_shape=(jax.Shap...  103 us
    pallas_call x1, Pallas kernels, body(): pl.pallas_call(functools.partial(finish, batch_rows), out_shape=(jax.Shap...  2.36 us

profile of v3, /device:TPU:1, one launch (start us, length us, event | category | flops | bytes accessed | tf_op | source)
XLA Modules:
  0.0 106.0 jit_solution(10283847333515794613)
XLA Ops:
  0.6 103.0 %swav.1 = (f32[2,384,128]{2,1,0:T(8,128)}, f32[512,256]{1,0:T(8,128)}) custom-call(bf16[2048,2,512]{2,1,0:T(2,128)(2,1)} %feats_in.1, bf16[512,256]{1,0:T(8,128)(2,1)} %weight_in.1, f32[375,256]{1,0:T(8,128)} %protos.1), custom_call_target="tpu_custom_call" | custom-call | tf_op jit(solution)/shard_map/swav/pallas_call | solution.py:523
  103.6 2.4 %finish.1 = (f32[375,256]{1,0:T(8,128)}, f32[512,256]{1,0:T(8,128)}, f32[1,1]{1,0:T(1,128)}) custom-call(f32[2,384,128]{2,1,0:T(8,128)} %get-tuple-element.8.fg, f32[512,256]{1,0:T(8,128)} %get-tuple-element.9.fw, f32[375,256]{1,0:T(8,128)} %protos.1), custom_call_target="tpu_custom_call" | custom-call | tf_op jit(solution)/shard_map/finish/pallas_call | solution.py:537

commit v4 on v3

--- a/solution.py
+++ b/solution.py
@@ -26,13 +26,17 @@
 WR = 256
 D = 256
 E = 512
-HALF = KP // 2
+NQ = 4
+QR = KP // NQ // NC
 DH = D // 2
 PR_ROWS = KP // NP
 GH = E // 2
 GR = GH // NP
 XY = [(dx, dy) for dx in range(NX) for dy in range(NY) if dx or dy]
 ZO = [1, 7, 2, 6, 3, 5, 4]
+FAR = [4, 3, 5, 2, 6]
+NEAR = [1, 7]
+NB = [(1, 0), (-1, 0), (0, 1)]
 
 
 def nt_dot(a, b):
@@ -52,7 +56,7 @@
     ex, sc, so, so_line, den, rsc, acc, vec, csum, cothers, gm,
     buf_a, buf_b, vec_b,
     eg, gm_line, col, lanes, share_z, pg, buf_p, pr, buf_q, fg, gw, buf_w, gwr, buf_x, buf_y, fw, loss_acc,
-    s_z, r_z, s_f, r_f, s_e, r_e, s_a, r_a, s_b, r_b, s_c, r_c,
+    s_z, r_z, s_n, r_n, s_f, r_f, s_e, r_e, s_a, r_a, s_b, r_b, s_c, r_c,
     s_l, r_l, s_v, r_v, s_h, r_h, s_p, r_p, s_q, r_q, s_qg, r_qg, s_qc, r_qc,
     s_w, r_w, s_wx, r_wx, s_wz, r_wz, s_wg, r_wg, s_wc, r_wc,
 ):
@@ -112,13 +116,19 @@
     pu[...] = jnp.zeros_like(pu)
     own = protos[...]
     pu[0:KS, :] = own * lax.rsqrt(jnp.sum(own * own, axis=-1, keepdims=True) + TINY)
-    ph[z] = pu[...].astype(BF)
+    ph[z] = pu[...].astype(BF).reshape(NQ, NC, QR, D)
     pl.semaphore_wait(barrier, 1 + len(XY) + len(ZO))
 
-    zcopies = {}
-    for i, dz in enumerate(ZO):
-        part = ph.at[z, pl.ds(pl.multiple_of(c * HALF, HALF), HALF)]
-        zcopies[dz] = send(part, part, s_z.at[i], r_z.at[i], z_dev(dz))
+    colour = (x + 2 * y) % NQ
+    for i, dz in enumerate(FAR):
+        part = ph.at[z, colour, c]
+        send(part, part, s_z.at[i], r_z.at[i], z_dev(dz))
+    for i, dz in enumerate(NEAR):
+        part = ph.at[z, :, c]
+        send(part, part, s_z.at[len(FAR) + i], r_z.at[len(FAR) + i], z_dev(dz))
+
+    def slab(q):
+        return ph[q].reshape(KP, D)
 
     loads[1].wait()
     loads[2].wait()
@@ -141,7 +151,7 @@
     ecopy.wait_recv()
 
     def scores_slab(q):
-        pq_ = ph[q]
+        pq_ = slab(q)
         tot = jnp.zeros((8, KP), F32)
         for b in range(2):
             s = nt_dot(emb[b * WR : (b + 1) * WR, :], pq_)
@@ -153,13 +163,33 @@
         acc[q] = tot
 
     scores_slab(z)
-    for i, dz in enumerate(ZO):
-        q = (z + NZ - dz) % NZ
-        zcopies[dz].wait_recv()
-        part = ph.at[q, pl.ds(pl.multiple_of(c * HALF, HALF), HALF)]
-        fwd = send(part, part, s_f.at[i], r_f.at[i], sibling)
-        fwd.wait_recv()
-        scores_slab(q)
+    came = [(z + NZ - dz) % NZ for dz in FAR + NEAR]
+    for i in range(len(FAR)):
+        part = ph.at[came[i], colour, c]
+        arrival(part, s_z.at[i], r_z.at[i]).wait_recv()
+        for n, (dx, dy) in enumerate(NB):
+            send(part, part, s_n.at[i, n], r_n.at[i, n], plane_dev(plane(dx, dy)))
+
+    def to_sibling(i):
+        part = ph.at[came[i], :, c]
+        return send(part, part, s_f.at[i], r_f.at[i], sibling)
+
+    forwards = {}
+    for i in (len(FAR), len(FAR) + 1):
+        arrival(ph.at[came[i], :, c], s_z.at[i], r_z.at[i]).wait_recv()
+        forwards[i] = to_sibling(i)
+    for i in (len(FAR), len(FAR) + 1):
+        forwards[i].wait_recv()
+        scores_slab(came[i])
+    for i in range(len(FAR) + 1):
+        if i < len(FAR):
+            for n, (dx, dy) in enumerate(NB):
+                part = ph.at[came[i], (colour + 3 * NQ - dx - 2 * dy) % NQ, c]
+                arrival(part, s_n.at[i, n], r_n.at[i, n]).wait_recv()
+            forwards[i] = to_sibling(i)
+        if i:
+            forwards[i - 1].wait_recv()
+            scores_slab(came[i - 1])
 
     lane = lax.broadcasted_iota(jnp.int32, (NT, 128), 1)
     row = lax.broadcasted_iota(jnp.int32, (NT, 128), 0)
@@ -195,7 +225,7 @@
 
     def other_view():
         def step(q, carry):
-            s = nt_dot(emb[2 * WR : 3 * WR, :], ph[q])
+            s = nt_dot(emb[2 * WR : 3 * WR, :], slab(q))
             ex[q, 2 * WR : 3 * WR, :] = jnp.exp(s * (1.0 / EPSILON_CODES))
             sc[q, WR : 2 * WR, :] = s
             return carry
@@ -244,7 +274,7 @@
 
     def line_scores(dz):
         slot = line_slot(dz)
-        s = nt_dot(ph[z], emb_line[slot])
+        s = nt_dot(slab(z), emb_line[slot])
         so_line[slot] = jnp.exp(s * (1.0 / SOFTMAX_TEMPER))
 
     eye = lax.broadcasted_iota(jnp.int32, (128, 128), 0) == lax.broadcasted_iota(jnp.int32, (128, 128), 1)
@@ -365,7 +395,7 @@
 
     grads = jnp.zeros((2 * WR, D), F32)
     for q in range(NZ):
-        grads = grads + dot(gm[q], ph[q])
+        grads = grads + dot(gm[q], slab(q))
     eg[...] = grads
     along = jnp.sum(unit[...] * eg[...], axis=-1, keepdims=True)
     graw = ((eg[...] - unit[...] * along) * inv[...]).astype(BF)
@@ -502,7 +532,7 @@
     vm = pltpu.VMEM
     scratch = [
         vm((WR, 2, E), BF), vm((2, WR, E), BF), vm((E, D), BF), vm((KS, D), F32), dma((3,)),
-        vm((KP, D), F32), vm((NZ, KP, D), BF), vm((2 * WR, D), F32), vm((2 * WR, 1), F32),
+        vm((KP, D), F32), vm((NZ, NQ, NC, QR, D), BF), vm((2 * WR, D), F32), vm((2 * WR, 1), F32),
         vm((3 * WR, D), BF), vm((NZ, 2 * WR, D), BF), vm((E, 2 * WR), BF),
         vm((NZ, 3 * WR, KP), F32), vm((NZ, 2 * WR, KP), F32), vm((NZ, 2 * WR, KP), F32), vm((NZ, KP, 2 * WR), F32),
         vm((2 * WR, 1), F32), vm((2 * WR, 1), F32), vm((NZ, 8, KP), F32), vm((3, NT, 128), F32), vm((3, NT, 128), F32),
@@ -512,7 +542,7 @@
         vm((KP, D), F32), vm((KP, DH), F32), vm((KP, DH), F32), vm((nxy, PR_ROWS, DH), F32), vm((NC, KP, DH), F32),
         vm((E, D), F32), vm((GH, D), F32), vm((GH, D), F32), vm((nxy, GR, D), F32), vm((NZ, GR, D), F32), vm((E, D), F32),
         vm((8, 128), F32),
-        dma((nz,)), dma((nz,)), dma((nz,)), dma((nz,)), dma, dma,
+        dma((nz,)), dma((nz,)), dma((len(FAR), len(NB))), dma((len(FAR), len(NB))), dma((nz,)), dma((nz,)), dma, dma,
         dma((3, nxy)), dma((3, nxy)), dma((3, nz)), dma((3, nz)), dma, dma,
         dma((4, 2)), dma((4, 2)), dma((nz,)), dma((NZ,)), dma((nz,)), dma((NZ,)), dma, dma,
         dma((nxy,)), dma((nxy,)), dma((nxy,)), dma((NP,)), dma, dma,

time: 106 us -> 97.4 us (0.919)
  Pallas kernels: 105 us -> 96.6 us
    pallas_call x1, Pallas kernels: 103 us -> 94.2 us  [body(): pl.pallas_call(functools.partial(kernel, batch_rows), out_shape=(jax.Shap...]
where the time goes in v4:
time: 97.4 us; the launch traced here: 97.3 us
  Pallas kernels  96.6 us (99%)
    pallas_call x1, Pallas kernels, body(): pl.pallas_call(functools.partial(kernel, batch_rows), out_shape=(jax.Shap...  94.2 us
    pallas_call x1, Pallas kernels, body(): pl.pallas_call(functools.partial(finish, batch_rows), out_shape=(jax.Shap...  2.36 us

profile of v4, /device:TPU:1, one launch (start us, length us, event | category | flops | bytes accessed | tf_op | source)
XLA Modules:
  0.0 97.3 jit_solution(9584874228537988613)
XLA Ops:
  0.6 94.2 %swav.1 = (f32[2,384,128]{2,1,0:T(8,128)}, f32[512,256]{1,0:T(8,128)}) custom-call(bf16[2048,2,512]{2,1,0:T(2,128)(2,1)} %feats_in.1, bf16[512,256]{1,0:T(8,128)(2,1)} %weight_in.1, f32[375,256]{1,0:T(8,128)} %protos.1), custom_call_target="tpu_custom_call" | custom-call | tf_op jit(solution)/shard_map/swav/pallas_call | solution.py:553
  94.9 2.4 %finish.1 = (f32[375,256]{1,0:T(8,128)}, f32[512,256]{1,0:T(8,128)}, f32[1,1]{1,0:T(1,128)}) custom-call(f32[2,384,128]{2,1,0:T(8,128)} %get-tuple-element.8.fg, f32[512,256]{1,0:T(8,128)} %get-tuple-element.9.fw, f32[375,256]{1,0:T(8,128)} %protos.1), custom_call_target="tpu_custom_call" | custom-call | tf_op jit(solution)/shard_map/finish/pallas_call | solution.py:567

commit v5 on v4

--- a/solution.py
+++ b/solution.py
@@ -31,7 +31,9 @@
 DH = D // 2
 PR_ROWS = KP // NP
 GH = E // 2
-GR = GH // NP
+NH = 1
+GQ = GH // NH
+GR = GQ // NP
 XY = [(dx, dy) for dx in range(NX) for dy in range(NY) if dx or dy]
 ZO = [1, 7, 2, 6, 3, 5, 4]
 FAR = [4, 3, 5, 2, 6]
@@ -55,10 +57,9 @@
     pu, ph, unit, inv, emb, emb_line, xt,
     ex, sc, so, so_line, den, rsc, acc, vec, csum, cothers, gm,
     buf_a, buf_b, vec_b,
-    eg, gm_line, col, lanes, share_z, pg, buf_p, pr, buf_q, fg, gw, buf_w, gwr, buf_x, buf_y, fw, loss_acc,
-    s_z, r_z, s_n, r_n, s_f, r_f, s_e, r_e, s_a, r_a, s_b, r_b, s_c, r_c,
-    s_l, r_l, s_v, r_v, s_h, r_h, s_p, r_p, s_q, r_q, s_qg, r_qg, s_qc, r_qc,
-    s_w, r_w, s_wx, r_wx, s_wz, r_wz, s_wg, r_wg, s_wc, r_wc,
+    eg, gm_line, col, lanes, share_z, pg, buf_p, pr, buf_q, fg, gw, buf_w, buf_x, buf_y, fw, loss_acc,
+    s_x1, s_x2, s_z1, s_z2, s_f, s_m,
+    r_z, r_n, r_f, r_e, r_a, r_b, r_c, r_l, r_v, r_h, r_p, r_q, r_qg, r_qc, r_w, r_wx, r_wz, r_wg, r_wc,
 ):
     dp = lax.axis_index("dp")
     z = lax.axis_index("mp")
@@ -66,7 +67,8 @@
     o = 1 - c
     me_p = x * NY + y
     gf = LOSS_FACTOR / (2.0 * batch_rows * SOFTMAX_TEMPER)
-    pending = []
+    pools = {"x1": s_x1, "x2": s_x2, "z1": s_z1, "z2": s_z2, "f": s_f, "m": s_m}
+    pending = {}
 
     def plane(dx, dy):
         px, py = (x + dx) % NX, (y + dy) % NY
@@ -80,22 +82,21 @@
 
     sibling = {"dp": dp + 1 - 2 * c, "mp": z}
 
-    def send(src, dst, ssem, rsem, device):
+    def send(src, dst, key, rsem, device):
+        if key in pending:
+            pending.pop(key).wait_send()
         copy = pltpu.make_async_remote_copy(
-            src_ref=src, dst_ref=dst, send_sem=ssem, recv_sem=rsem, device_id=device, device_id_type=MESH
+            src_ref=src, dst_ref=dst, send_sem=pools[key[0]].at[key[1]], recv_sem=rsem,
+            device_id=device, device_id_type=MESH,
         )
         copy.start()
-        pending.append(copy)
+        pending[key] = copy
         return copy
 
-    def arrival(dst, ssem, rsem):
+    def arrival(dst, rsem):
         return pltpu.make_async_remote_copy(
-            src_ref=dst, dst_ref=dst, send_sem=ssem, recv_sem=rsem, device_id=sibling, device_id_type=MESH
+            src_ref=dst, dst_ref=dst, send_sem=s_m.at[0], recv_sem=rsem, device_id=sibling, device_id_type=MESH
         )
-
-    def wz_recv(dz):
-        k = (z + dz) % NZ
-        return arrival(buf_y.at[k], s_wz.at[0], r_wz.at[k])
 
     barrier = pltpu.get_barrier_semaphore()
     pl.semaphore_signal(barrier, inc=1, device_id=sibling, device_id_type=MESH)
@@ -122,10 +123,10 @@
     colour = (x + 2 * y) % NQ
     for i, dz in enumerate(FAR):
         part = ph.at[z, colour, c]
-        send(part, part, s_z.at[i], r_z.at[i], z_dev(dz))
+        send(part, part, ("z1", i), r_z.at[i], z_dev(dz))
     for i, dz in enumerate(NEAR):
         part = ph.at[z, :, c]
-        send(part, part, s_z.at[len(FAR) + i], r_z.at[len(FAR) + i], z_dev(dz))
+        send(part, part, ("z1", len(FAR) + i), r_z.at[len(FAR) + i], z_dev(dz))
 
     def slab(q):
         return ph[q].reshape(KP, D)
@@ -146,7 +147,7 @@
         emb[erow : erow + WR, :] = u.astype(BF)
 
     embed(o, WR, 2 * WR)
-    ecopy = send(emb.at[pl.ds(2 * WR, WR)], emb.at[pl.ds(WR, WR)], s_e, r_e, sibling)
+    ecopy = send(emb.at[pl.ds(2 * WR, WR)], emb.at[pl.ds(WR, WR)], ("m", 0), r_e, sibling)
     embed(c, 0, 0)
     ecopy.wait_recv()
 
@@ -166,17 +167,17 @@
     came = [(z + NZ - dz) % NZ for dz in FAR + NEAR]
     for i in range(len(FAR)):
         part = ph.at[came[i], colour, c]
-        arrival(part, s_z.at[i], r_z.at[i]).wait_recv()
+        arrival(part, r_z.at[i]).wait_recv()
         for n, (dx, dy) in enumerate(NB):
-            send(part, part, s_n.at[i, n], r_n.at[i, n], plane_dev(plane(dx, dy)))
+            send(part, part, ("x2", i * len(NB) + n), r_n.at[i, n], plane_dev(plane(dx, dy)))
 
     def to_sibling(i):
         part = ph.at[came[i], :, c]
-        return send(part, part, s_f.at[i], r_f.at[i], sibling)
+        return send(part, part, ("f", i), r_f.at[i], sibling)
 
     forwards = {}
     for i in (len(FAR), len(FAR) + 1):
-        arrival(ph.at[came[i], :, c], s_z.at[i], r_z.at[i]).wait_recv()
+        arrival(ph.at[came[i], :, c], r_z.at[i]).wait_recv()
         forwards[i] = to_sibling(i)
     for i in (len(FAR), len(FAR) + 1):
         forwards[i].wait_recv()
@@ -185,7 +186,7 @@
         if i < len(FAR):
             for n, (dx, dy) in enumerate(NB):
                 part = ph.at[came[i], (colour + 3 * NQ - dx - 2 * dy) % NQ, c]
-                arrival(part, s_n.at[i, n], r_n.at[i, n]).wait_recv()
+                arrival(part, r_n.at[i, n]).wait_recv()
             forwards[i] = to_sibling(i)
         if i:
             forwards[i - 1].wait_recv()
@@ -206,20 +207,20 @@
         copies = []
         for i, (dx, dy) in enumerate(XY):
             copies.append(
-                send(vec.at[k], buf_a.at[k, i], s_a.at[k, i], r_a.at[k, i], plane_dev(plane(dx, dy)))
+                send(vec.at[k], buf_a.at[k, i], ("x1", i), r_a.at[k], plane_dev(plane(dx, dy)))
             )
         work_a()
         total = vec[k]
-        for i, copy in enumerate(copies):
-            copy.wait_recv()
+        arrival(buf_a.at[k], r_a.at[k]).wait_recv()
+        for i in range(len(XY)):
             total = total + buf_a[k, i]
         vec_b[k] = total
         copies = []
         for i, dz in enumerate(ZO):
-            copies.append(send(vec_b.at[k], buf_b.at[k, i], s_b.at[k, i], r_b.at[k, i], z_dev(dz)))
+            copies.append(send(vec_b.at[k], buf_b.at[k, i], ("z1", i), r_b.at[k], z_dev(dz)))
         work_b()
-        for i, copy in enumerate(copies):
-            copy.wait_recv()
+        arrival(buf_b.at[k], r_b.at[k]).wait_recv()
+        for i in range(len(ZO)):
             total = total + buf_b[k, i]
         csum[k] = jnp.where(valid, 1.0 / total, 0.0)
 
@@ -262,7 +263,7 @@
             part = emb_line.at[slot]
             if n == NZ // 2:
                 part = emb_line.at[slot, pl.ds(i * WR, WR)]
-            send(part, part, s_l.at[n - 1, i], r_l.at[n - 1, i], z_dev(way % NZ))
+            send(part, part, ("m", 2 + i), r_l.at[n - 1, i], z_dev(way % NZ))
 
     def line_wait(n):
         for i, way in enumerate((1, -1)):
@@ -270,7 +271,7 @@
             part = emb_line.at[slot]
             if n == NZ // 2:
                 part = emb_line.at[slot, pl.ds(i * WR, WR)]
-            arrival(part, s_l.at[n - 1, i], r_l.at[n - 1, i]).wait_recv()
+            arrival(part, r_l.at[n - 1, i]).wait_recv()
 
     def line_scores(dz):
         slot = line_slot(dz)
@@ -283,10 +284,6 @@
         for i in range(2 * WR // 128):
             part = jnp.broadcast_to(ref[i * 128 : (i + 1) * 128, :], (128, 128))
             lanes[z, row + i : row + i + 1, :] = jnp.sum(jnp.where(eye, part, 0.0), axis=0, keepdims=True)
-
-    def transposes_x():
-        xt[:, 0:WR] = feats[c].astype(F32).T.astype(BF)
-        xt[:, WR : 2 * WR] = feats[o].astype(F32).T.astype(BF)
 
     def row_inverse(cs, rows, R):
         total = jnp.zeros((R, 128), F32)
@@ -297,7 +294,7 @@
         return 1.0 / jnp.sum(total, axis=1, keepdims=True)
 
     def sinkhorn_pass(k):
-        R = 64
+        R = 128
         acc[...] = jnp.zeros_like(acc)
 
         def step(b, carry):
@@ -327,19 +324,26 @@
         to_lanes(den, 4)
 
     def work_3a():
-        transposes_x()
         line_scores(-2)
 
-    reduce_columns(0, work_1a, lambda: denominators(0))
+    def work_1b():
+        denominators(0)
+        xt[:, 0:WR] = feats[c].astype(F32).T.astype(BF)
+
+    def work_2a():
+        denominators(WR)
+        xt[:, WR : 2 * WR] = feats[o].astype(F32).T.astype(BF)
+
+    reduce_columns(0, work_1a, work_1b)
     line_wait(1)
     line_step(2)
     sinkhorn_pass(0)
-    reduce_columns(1, lambda: denominators(WR), work_2b)
+    reduce_columns(1, work_2a, work_2b)
     line_wait(2)
     line_step(3)
     sinkhorn_pass(1)
     reduce_columns(2, work_3a, lambda: line_scores(2))
-    ccopy = send(csum.at[2], cothers, s_c, r_c, sibling)
+    ccopy = send(csum.at[2], cothers, ("m", 1), r_c, sibling)
     line_wait(3)
     line_step(4)
 
@@ -357,9 +361,7 @@
     row_scales(cothers, WR, 2 * WR)
     to_lanes(rsc, 0)
     for i, dz in enumerate(ZO):
-        send(lanes.at[z], lanes.at[z], s_v.at[i], r_v.at[z], z_dev(dz))
-    line_scores(-3)
-    line_scores(3)
+        send(lanes.at[z], lanes.at[z], ("z1", i), r_v.at[z], z_dev(dz))
 
     RG = 32
     loss_acc[...] = jnp.zeros_like(loss_acc)
@@ -379,8 +381,8 @@
                 cols = slice(j * 128, (j + 1) * 128)
                 ac = ex[q, rows_c, cols] * csum[2, t : t + 1, :] * rc
                 ao = ex[q, erows_o, cols] * cothers[t : t + 1, :] * ro
-                gm[q, rows_c, cols] = (so[q, rows_c, cols] * dc - ao).astype(BF)
-                gm[q, rows_o, cols] = (so[q, rows_o, cols] * do - ac).astype(BF)
+                gm[rows_c, t * 128 : (t + 1) * 128] = (so[q, rows_c, cols] * dc - ao).astype(BF)
+                gm[rows_o, t * 128 : (t + 1) * 128] = (so[q, rows_o, cols] * do - ac).astype(BF)
                 total = total + ao * sc[q, rows_c, cols] + ac * sc[q, rows_o, cols]
         loss_acc[...] += jnp.sum(total.reshape(RG // 8, 8, 128), axis=0)
         return carry
@@ -391,35 +393,46 @@
     share = jnp.sum(loss_acc[...]) * (1.0 / (SOFTMAX_TEMPER * gf)) - log_total
     share_z[z] = jnp.full((8, 128), share, F32)
     for i, dz in enumerate(ZO):
-        send(share_z.at[z], share_z.at[z], s_h.at[i], r_h.at[z], z_dev(dz))
-
-    grads = jnp.zeros((2 * WR, D), F32)
-    for q in range(NZ):
-        grads = grads + dot(gm[q], slab(q))
-    eg[...] = grads
+        send(share_z.at[z], share_z.at[z], ("z2", i), r_h.at[z], z_dev(dz))
+
+    eg[...] = dot(gm[...], ph[...].reshape(NZ * KP, D))
     along = jnp.sum(unit[...] * eg[...], axis=-1, keepdims=True)
     graw = ((eg[...] - unit[...] * along) * inv[...]).astype(BF)
-    gw[...] = dot(xt[...], graw)
-    wcopy = send(gw.at[pl.ds(pl.multiple_of(o * GH, GH), GH)], buf_w, s_w, r_w, sibling)
-    wcopy.wait_recv()
-    gwr[...] = gw[pl.ds(pl.multiple_of(c * GH, GH), GH), :] + buf_w[...]
+    def half_rows(h, core):
+        return pl.ds(pl.multiple_of((h * NC + core) * GQ, GQ), GQ)
+
+    def own_rows(h, p):
+        return pl.ds(pl.multiple_of((h * NC + c) * GQ + p * GR, GR), GR)
+
+    wcopy = []
+    for h in range(NH):
+        theirs = half_rows(h, o)
+        gw[theirs, :] = dot(xt[theirs, :], graw)
+        wcopy.append(send(gw.at[theirs], buf_w.at[h], ("m", 6 + 2 * h), r_w.at[h], sibling))
     wcopies = []
-    for i, (dx, dy) in enumerate(XY):
-        p = plane(dx, dy)
-        wcopies.append(
-            send(gwr.at[pl.ds(pl.multiple_of(p * GR, GR), GR)], buf_x.at[i], s_wx.at[i], r_wx.at[i], plane_dev(p))
-        )
+    for h in range(NH):
+        ours = half_rows(h, c)
+        grads = dot(xt[ours, :], graw)
+        wcopy[h].wait_recv()
+        gw[ours, :] = grads + buf_w[h]
+        for i, (dx, dy) in enumerate(XY):
+            p = plane(dx, dy)
+            wcopies.append(
+                send(gw.at[own_rows(h, p)], buf_x.at[h, i], ("x1", i), r_wx.at[h], plane_dev(p))
+            )
 
     for v, cs in enumerate((csum.at[2], cothers)):
         for j in range(LT):
             part = jnp.broadcast_to(cs[pl.ds(z * LT + j, 1), :], (128, 128))
             part = jnp.sum(jnp.where(eye, part, 0.0), axis=1, keepdims=True)
             col[v, j * 128 : (j + 1) * 128, :] = jnp.broadcast_to(part, (128, 128))
+    line_scores(-3)
+    line_scores(3)
     line_wait(4)
     line_scores(4)
     for dz in ZO:
         k = line_slot(dz)
-        arrival(lanes.at[k], s_v.at[0], r_v.at[k]).wait_recv()
+        arrival(lanes.at[k], r_v.at[k]).wait_recv()
 
     def line_grad(k, carry):
         scale = [lanes[k, i : i + 1, :] * gf for i in range(4)]
@@ -443,73 +456,75 @@
     pg[...] = grads
     for dz in ZO:
         k = line_slot(dz)
-        arrival(share_z.at[k], s_h.at[0], r_h.at[k]).wait_recv()
+        arrival(share_z.at[k], r_h.at[k]).wait_recv()
     share = share_z[0, 0:1, 0:1]
     for k in range(1, NZ):
         share = share + share_z[k, 0:1, 0:1]
     spare = lax.broadcasted_iota(jnp.int32, (8, D), 0) == 7
     pg[KP - 8 : KP, :] = jnp.where(spare, share, pg[KP - 8 : KP, :])
-    pcopy = send(pg.at[:, pl.ds(pl.multiple_of(o * DH, DH), DH)], buf_p, s_p, r_p, sibling)
+    pcopy = send(pg.at[:, pl.ds(pl.multiple_of(o * DH, DH), DH)], buf_p, ("m", 4), r_p, sibling)
     pcopy.wait_recv()
     pr[...] = pg[:, pl.ds(pl.multiple_of(c * DH, DH), DH)] + buf_p[...]
     qcopies = []
     for i, (dx, dy) in enumerate(XY):
         p = plane(dx, dy)
         qcopies.append(
-            send(pr.at[pl.ds(pl.multiple_of(p * PR_ROWS, PR_ROWS), PR_ROWS)], buf_q.at[i], s_q.at[i], r_q.at[i], plane_dev(p))
+            send(pr.at[pl.ds(pl.multiple_of(p * PR_ROWS, PR_ROWS), PR_ROWS)], buf_q.at[i], ("x2", i), r_q, plane_dev(p))
         )
 
-    total = gwr[pl.ds(pl.multiple_of(me_p * GR, GR), GR), :]
-    for i, copy in enumerate(wcopies):
-        copy.wait_recv()
-        total = total + buf_x[i]
-    buf_y[z] = total
-    wz = []
-    for i, dz in enumerate(ZO):
-        wz.append(send(buf_y.at[z], buf_y.at[z], s_wz.at[i], r_wz.at[z], z_dev(dz)))
-
-    mine = pl.ds(pl.multiple_of(me_p * PR_ROWS, PR_ROWS), PR_ROWS)
-    total = pr[mine, :]
-    for i, copy in enumerate(qcopies):
-        copy.wait_recv()
+    for h in range(NH):
+        total = gw[own_rows(h, me_p), :]
+        arrival(buf_x.at[h], r_wx.at[h]).wait_recv()
+        for i in range(len(XY)):
+            total = total + buf_x[h, i]
+        buf_y[h, z] = total
+        for i, dz in enumerate(ZO):
+            send(buf_y.at[h, z], buf_y.at[h, z], ("z1", i), r_wz.at[h, z], z_dev(dz))
+
+    mine_p = pl.ds(pl.multiple_of(me_p * PR_ROWS, PR_ROWS), PR_ROWS)
+    total = pr[mine_p, :]
+    arrival(buf_q, r_q).wait_recv()
+    for i in range(len(XY)):
         total = total + buf_q[i]
-    fg[c, mine, :] = total
+    fg[c, mine_p, :] = total
     for i, (dx, dy) in enumerate(XY):
-        send(fg.at[c, mine], fg.at[c, mine], s_qg.at[i], r_qg.at[me_p], plane_dev(plane(dx, dy)))
-
-    for dz in ZO:
-        wz_recv(dz).wait_recv()
-    total = buf_y[0]
-    for k in range(1, NZ):
-        total = total + buf_y[k]
-    mine = pl.ds(pl.multiple_of(c * GH + me_p * GR, GR), GR)
-    fw[mine, :] = total
-    wg = []
-    for i, (dx, dy) in enumerate(XY):
-        wg.append(
-            send(fw.at[mine], fw.at[mine], s_wg.at[i], r_wg.at[me_p], plane_dev(plane(dx, dy)))
-        )
+        send(fg.at[c, mine_p], fg.at[c, mine_p], ("x2", i), r_qg.at[me_p], plane_dev(plane(dx, dy)))
+
+    for h in range(NH):
+        for dz in ZO:
+            k = line_slot(dz)
+            arrival(buf_y.at[h, k], r_wz.at[h, k]).wait_recv()
+        total = buf_y[h, 0]
+        for k in range(1, NZ):
+            total = total + buf_y[h, k]
+        part = own_rows(h, me_p)
+        fw[part, :] = total
+        for i, (dx, dy) in enumerate(XY):
+            send(fw.at[part], fw.at[part], ("x1", i), r_wg.at[h, me_p], plane_dev(plane(dx, dy)))
 
     for dx, dy in XY:
         p = plane(dx, dy)
-        part = pl.ds(pl.multiple_of(p * PR_ROWS, PR_ROWS), PR_ROWS)
-        arrival(fg.at[c, part], s_qg.at[0], r_qg.at[p]).wait_recv()
-    qc = send(fg.at[c], fg.at[c], s_qc, r_qc, sibling)
-    qc.wait_recv()
-    for dx, dy in XY:
-        p = plane(dx, dy)
-        arrival(fw.at[pl.ds(pl.multiple_of(c * GH + p * GR, GR), GR)], s_wg.at[0], r_wg.at[p]).wait_recv()
-    half = pl.ds(pl.multiple_of(c * GH, GH), GH)
-    wc = send(fw.at[half], fw.at[half], s_wc, r_wc, sibling)
-    wc.wait_recv()
+        part = fg.at[c, pl.ds(pl.multiple_of(p * PR_ROWS, PR_ROWS), PR_ROWS)]
+        arrival(part, r_qg.at[p]).wait_recv()
+    send(fg.at[c], fg.at[c], ("m", 5), r_qc, sibling).wait_recv()
     out_f = pltpu.make_async_copy(fg, gproto_out, s_in.at[0])
+    out_f.start()
+
+    forwards = []
+    for h in range(NH):
+        for i, (dx, dy) in enumerate(XY):
+            p = plane(dx, dy)
+            arrival(fw.at[own_rows(h, p)], r_wg.at[h, p]).wait_recv()
+        part = fw.at[half_rows(h, c)]
+        forwards.append(send(part, part, ("m", 7 + 2 * h), r_wc.at[h], sibling))
+    for copy in forwards:
+        copy.wait_recv()
     out_w = pltpu.make_async_copy(fw, gweight_out, s_in.at[1])
-    out_f.start()
     out_w.start()
     out_f.wait()
     out_w.wait()
 
-    for copy in pending:
+    for copy in pending.values():
         copy.wait_send()
 
 
@@ -536,17 +551,15 @@
         vm((3 * WR, D), BF), vm((NZ, 2 * WR, D), BF), vm((E, 2 * WR), BF),
         vm((NZ, 3 * WR, KP), F32), vm((NZ, 2 * WR, KP), F32), vm((NZ, 2 * WR, KP), F32), vm((NZ, KP, 2 * WR), F32),
         vm((2 * WR, 1), F32), vm((2 * WR, 1), F32), vm((NZ, 8, KP), F32), vm((3, NT, 128), F32), vm((3, NT, 128), F32),
-        vm((NT, 128), F32), vm((NZ, 2 * WR, KP), BF),
+        vm((NT, 128), F32), vm((2 * WR, NZ * KP), BF),
         vm((3, nxy, NT, 128), F32), vm((3, nz, NT, 128), F32), vm((3, NT, 128), F32),
         vm((2 * WR, D), F32), vm((NZ, KP, 2 * WR), BF), vm((2, KP, 128), F32), vm((NZ, 8, 128), F32), vm((NZ, 8, 128), F32),
         vm((KP, D), F32), vm((KP, DH), F32), vm((KP, DH), F32), vm((nxy, PR_ROWS, DH), F32), vm((NC, KP, DH), F32),
-        vm((E, D), F32), vm((GH, D), F32), vm((GH, D), F32), vm((nxy, GR, D), F32), vm((NZ, GR, D), F32), vm((E, D), F32),
+        vm((E, D), F32), vm((NH, GQ, D), F32), vm((NH, nxy, GR, D), F32), vm((NH, NZ, GR, D), F32), vm((E, D), F32),
         vm((8, 128), F32),
-        dma((nz,)), dma((nz,)), dma((len(FAR), len(NB))), dma((len(FAR), len(NB))), dma((nz,)), dma((nz,)), dma, dma,
-        dma((3, nxy)), dma((3, nxy)), dma((3, nz)), dma((3, nz)), dma, dma,
-        dma((4, 2)), dma((4, 2)), dma((nz,)), dma((NZ,)), dma((nz,)), dma((NZ,)), dma, dma,
-        dma((nxy,)), dma((nxy,)), dma((nxy,)), dma((NP,)), dma, dma,
-        dma, dma, dma((nxy,)), dma((nxy,)), dma((nz,)), dma((NZ,)), dma((nxy,)), dma((NP,)), dma, dma,
+        dma((nxy,)), dma((nxy,)), dma((nz,)), dma((nz,)), dma((nz,)), dma((6 + 2 * NH,)),
+        dma((nz,)), dma((len(FAR), len(NB))), dma((nz,)), dma, dma((3,)), dma((3,)), dma, dma((4, 2)), dma((NZ,)),
+        dma((NZ,)), dma, dma, dma((NP,)), dma, dma((NH,)), dma((NH,)), dma((NH, NZ)), dma((NH, NP)), dma((NH,)),
     ]
     vspec = pl.BlockSpec(memory_space=pltpu.VMEM)
     aspec = pl.BlockSpec(memory_space=pl.ANY)

time: 97.4 us -> 95 us (0.975)
  Pallas kernels: 96.6 us -> 94.2 us
    pallas_call x1, Pallas kernels: 94.2 us -> 91.8 us  [body(): pl.pallas_call(functools.partial(kernel, batch_rows), out_shape=(jax.Shap...]
where the time goes in v5:
time: 95 us; the launch traced here: 94.8 us
  Pallas kernels  94.2 us (99%)
    pallas_call x1, Pallas kernels, body(): pl.pallas_call(functools.partial(kernel, batch_rows), out_shape=(jax.Shap...  91.8 us
    pallas_call x1, Pallas kernels, body(): pl.pallas_call(functools.partial(finish, batch_rows), out_shape=(jax.Shap...  2.36 us

profile of v5, /device:TPU:1, one launch (start us, length us, event | category | flops | bytes accessed | tf_op | source)
XLA Modules:
  0.0 94.8 jit_solution(4574553399491336088)
XLA Ops:
  0.6 91.8 %swav.1 = (f32[2,384,128]{2,1,0:T(8,128)}, f32[512,256]{1,0:T(8,128)}) custom-call(bf16[2048,2,512]{2,1,0:T(2,128)(2,1)} %feats_in.1, bf16[512,256]{1,0:T(8,128)(2,1)} %weight_in.1, f32[375,256]{1,0:T(8,128)} %protos.1), custom_call_target="tpu_custom_call" | custom-call | tf_op jit(solution)/shard_map/swav/pallas_call | solution.py:566
  92.5 2.4 %finish.1 = (f32[375,256]{1,0:T(8,128)}, f32[512,256]{1,0:T(8,128)}, f32[1,1]{1,0:T(1,128)}) custom-call(f32[2,384,128]{2,1,0:T(8,128)} %get-tuple-element.8.fg, f32[512,256]{1,0:T(8,128)} %get-tuple-element.9.fw, f32[375,256]{1,0:T(8,128)} %protos.1), custom_call_target="tpu_custom_call" | custom-call | tf_op jit(solution)/shard_map/finish/pallas_call | solution.py:580

commit v6 on v5

--- a/solution.py
+++ b/solution.py
@@ -349,19 +349,19 @@
 
     def row_scales(cs, row, erow):
         def step(b, carry):
-            R = 64
+            R = 128
             rows = pl.ds(pl.multiple_of(row + b * R, R), R)
             rsc[rows, :] = row_inverse(cs, pl.ds(pl.multiple_of(erow + b * R, R), R), R)
             return carry
 
-        lax.fori_loop(0, WR // 64, step, 0)
+        lax.fori_loop(0, WR // 128, step, 0)
 
     row_scales(csum.at[2], 0, 0)
     ccopy.wait_recv()
     row_scales(cothers, WR, 2 * WR)
     to_lanes(rsc, 0)
     for i, dz in enumerate(ZO):
-        send(lanes.at[z], lanes.at[z], ("z1", i), r_v.at[z], z_dev(dz))
+        send(lanes.at[z], lanes.at[z], ("z1", i), r_v, z_dev(dz))
 
     RG = 32
     loss_acc[...] = jnp.zeros_like(loss_acc)
@@ -393,7 +393,7 @@
     share = jnp.sum(loss_acc[...]) * (1.0 / (SOFTMAX_TEMPER * gf)) - log_total
     share_z[z] = jnp.full((8, 128), share, F32)
     for i, dz in enumerate(ZO):
-        send(share_z.at[z], share_z.at[z], ("z2", i), r_h.at[z], z_dev(dz))
+        send(share_z.at[z], share_z.at[z], ("z2", i), r_h, z_dev(dz))
 
     eg[...] = dot(gm[...], ph[...].reshape(NZ * KP, D))
     along = jnp.sum(unit[...] * eg[...], axis=-1, keepdims=True)
@@ -430,9 +430,7 @@
     line_scores(3)
     line_wait(4)
     line_scores(4)
-    for dz in ZO:
-        k = line_slot(dz)
-        arrival(lanes.at[k], r_v.at[k]).wait_recv()
+    arrival(lanes.at[pl.ds(0, NZ - 1)], r_v).wait_recv()
 
     def line_grad(k, carry):
         scale = [lanes[k, i : i + 1, :] * gf for i in range(4)]
@@ -454,9 +452,7 @@
     for k in range(NZ):
         grads = grads + dot(gm_line[k], emb_line[k])
     pg[...] = grads
-    for dz in ZO:
-        k = line_slot(dz)
-        arrival(share_z.at[k], r_h.at[k]).wait_recv()
+    arrival(share_z.at[pl.ds(0, NZ - 1)], r_h).wait_recv()
     share = share_z[0, 0:1, 0:1]
     for k in range(1, NZ):
         share = share + share_z[k, 0:1, 0:1]
@@ -479,7 +475,7 @@
             total = total + buf_x[h, i]
         buf_y[h, z] = total
         for i, dz in enumerate(ZO):
-            send(buf_y.at[h, z], buf_y.at[h, z], ("z1", i), r_wz.at[h, z], z_dev(dz))
+            send(buf_y.at[h, z], buf_y.at[h, z], ("z1", i), r_wz.at[h], z_dev(dz))
 
     mine_p = pl.ds(pl.multiple_of(me_p * PR_ROWS, PR_ROWS), PR_ROWS)
     total = pr[mine_p, :]
@@ -488,33 +484,26 @@
         total = total + buf_q[i]
     fg[c, mine_p, :] = total
     for i, (dx, dy) in enumerate(XY):
-        send(fg.at[c, mine_p], fg.at[c, mine_p], ("x2", i), r_qg.at[me_p], plane_dev(plane(dx, dy)))
+        send(fg.at[c, mine_p], fg.at[c, mine_p], ("x2", i), r_qg, plane_dev(plane(dx, dy)))
 
     for h in range(NH):
-        for dz in ZO:
-            k = line_slot(dz)
-            arrival(buf_y.at[h, k], r_wz.at[h, k]).wait_recv()
+        arrival(buf_y.at[h, pl.ds(0, NZ - 1)], r_wz.at[h]).wait_recv()
         total = buf_y[h, 0]
         for k in range(1, NZ):
             total = total + buf_y[h, k]
         part = own_rows(h, me_p)
         fw[part, :] = total
         for i, (dx, dy) in enumerate(XY):
-            send(fw.at[part], fw.at[part], ("x1", i), r_wg.at[h, me_p], plane_dev(plane(dx, dy)))
-
-    for dx, dy in XY:
-        p = plane(dx, dy)
-        part = fg.at[c, pl.ds(pl.multiple_of(p * PR_ROWS, PR_ROWS), PR_ROWS)]
-        arrival(part, r_qg.at[p]).wait_recv()
+            send(fw.at[part], fw.at[part], ("x1", i), r_wg.at[h], plane_dev(plane(dx, dy)))
+
+    arrival(buf_q, r_qg).wait_recv()
     send(fg.at[c], fg.at[c], ("m", 5), r_qc, sibling).wait_recv()
     out_f = pltpu.make_async_copy(fg, gproto_out, s_in.at[0])
     out_f.start()
 
     forwards = []
     for h in range(NH):
-        for i, (dx, dy) in enumerate(XY):
-            p = plane(dx, dy)
-            arrival(fw.at[own_rows(h, p)], r_wg.at[h, p]).wait_recv()
+        arrival(buf_x.at[h], r_wg.at[h]).wait_recv()
         part = fw.at[half_rows(h, c)]
         forwards.append(send(part, part, ("m", 7 + 2 * h), r_wc.at[h], sibling))
     for copy in forwards:
@@ -558,8 +547,8 @@
         vm((E, D), F32), vm((NH, GQ, D), F32), vm((NH, nxy, GR, D), F32), vm((NH, NZ, GR, D), F32), vm((E, D), F32),
         vm((8, 128), F32),
         dma((nxy,)), dma((nxy,)), dma((nz,)), dma((nz,)), dma((nz,)), dma((6 + 2 * NH,)),
-        dma((nz,)), dma((len(FAR), len(NB))), dma((nz,)), dma, dma((3,)), dma((3,)), dma, dma((4, 2)), dma((NZ,)),
-        dma((NZ,)), dma, dma, dma((NP,)), dma, dma((NH,)), dma((NH,)), dma((NH, NZ)), dma((NH, NP)), dma((NH,)),
+        dma((nz,)), dma((len(FAR), len(NB))), dma((nz,)), dma, dma((3,)), dma((3,)), dma, dma((4, 2)), dma,
+        dma, dma, dma, dma, dma, dma((NH,)), dma((NH,)), dma((NH,)), dma((NH,)), dma((NH,)),
     ]
     vspec = pl.BlockSpec(memory_space=pltpu.VMEM)
     aspec = pl.BlockSpec(memory_space=pl.ANY)

time: 95 us -> 94.4 us (level)
  no operation moved by 1% of the time
where the time goes in v6:
time: 94.4 us; the launch traced here: 94.3 us
  Pallas kernels  93.6 us (99%)
    pallas_call x1, Pallas kernels, body(): pl.pallas_call(functools.partial(kernel, batch_rows), out_shape=(jax.Shap...  91.3 us
    pallas_call x1, Pallas kernels, body(): pl.pallas_call(functools.partial(finish, batch_rows), out_shape=(jax.Shap...  2.36 us

profile of v6, /device:TPU:1, one launch (start us, length us, event | category | flops | bytes accessed | tf_op | source)
XLA Modules:
  0.0 94.3 jit_solution(10553697890690038884)
XLA Ops:
  0.6 91.3 %swav.1 = (f32[2,384,128]{2,1,0:T(8,128)}, f32[512,256]{1,0:T(8,128)}) custom-call(bf16[2048,2,512]{2,1,0:T(2,128)(2,1)} %feats_in.1, bf16[512,256]{1,0:T(8,128)(2,1)} %weight_in.1, f32[375,256]{1,0:T(8,128)} %protos.1), custom_call_target="tpu_custom_call" | custom-call | tf_op jit(solution)/shard_map/swav/pallas_call | solution.py:555
  91.9 2.4 %finish.1 = (f32[375,256]{1,0:T(8,128)}, f32[512,256]{1,0:T(8,128)}, f32[1,1]{1,0:T(1,128)}) custom-call(f32[2,384,128]{2,1,0:T(8,128)} %get-tuple-element.8.fg, f32[512,256]{1,0:T(8,128)} %get-tuple-element.9.fw, f32[375,256]{1,0:T(8,128)} %protos.1), custom_call_target="tpu_custom_call" | custom-call | tf_op jit(solution)/shard_map/finish/pallas_call | solution.py:569
